TPU v7x, 256 devices: a whole 4x4x8 slice. The times are simulated.
256 devices in a mesh: dp: 128 (over y, z, x), mp: 2 (over core).
Axes of the slice: x: 4, y: 4, z: 8, core: 2. Of those that a mesh axis runs over, the one named last changes fastest.
Arguments:
- features: bfloat16 [32768, 768], P('dp', 'mp'), may hold values from -0.21875 to 0.21875
- labels: int32 [32768], P('dp'), may hold values from 0 to 131071, as said below
- queries: bfloat16 [32768, 768], P('dp', 'mp'), may hold values from -240 to 240
- bank: float32 [131072, 768], P('dp', 'mp'), may hold values from -0.21875 to 0.21875
- old_conc: float32 [131072], P('dp'), may hold values from 0.4 to 0.6
- neg_index: int32 [8192], replicated, may hold values from 0 to 131071, as said below
Outputs:
- new_bank: float32 [131072, 768], P('dp', 'mp')
- new_conc: float32 [131072], P('dp')
- loss: float32 [32768], P('dp')
- grad: float32 [32768, 768], P('dp', 'mp')
Inputs may be any that keep to these rules, and one draw needn't show every extreme that they name: In each aligned block of 256 rows, at most 6 labels fall in any one range of 1024 consecutive prototypes starting at a multiple of 1024; one such range receives exactly 6 labels from every block. `neg_index`: entries j * 64 to (j + 1) * 64 - 1 are distinct prototypes of the range j * 1024 to (j + 1) * 1024 - 1.
All inputs are finite; a program needn't handle non-finite values.
Results may differ from a plain program's by a relative error of at most 0.0074.
Values may be sent and summed in bfloat16 or wider, within the bound.
A program may use at most 64 MiB of HBM per device.

v0:
```python
import jax
import jax.numpy as jnp
from jax import lax
from jax.sharding import PartitionSpec as P


def sent_to_all(value, axis):
    copies = jnp.broadcast_to(value, (lax.axis_size(axis), *value.shape))
    return lax.all_to_all(copies, axis, split_axis=0, concat_axis=0, tiled=True)


def laid_out(parts, dim):
    dims = list(parts.shape[1:])
    dims[dim] *= parts.shape[0]
    return jnp.moveaxis(parts, 0, dim).reshape(dims)


def gather_directly(value, axis, dim):
    parts = sent_to_all(value, axis)
    return laid_out(parts, dim)


def taken_together(value, axis):
    everything = sent_to_all(value, axis)
    return jnp.sum(everything, axis=0)


def all_in_one(value, axis):
    leaves = jax.tree.leaves(value)
    sequence = sorted(range(len(leaves)), key=lambda k: -leaves[k].size)
    width = (1, *leaves[sequence[0]].shape)[-1]
    lines = [
        jnp.pad(leaves[k].reshape(-1), (0, -leaves[k].size % width)).reshape(-1, width)
        for k in sequence
    ]
    both, at, found = (lax.all_gather(jnp.concatenate(lines), axis), 0, {})
    for k, line in zip(sequence, lines):
        share = both[:, at : at + len(line)].reshape(len(both), -1)
        found[k] = share[:, : leaves[k].size].reshape(-1, *leaves[k].shape)
        at += len(line)
    numbers = iter(range(len(leaves)))
    return jax.tree.map(lambda _: found[next(numbers)], value)


def combined_all(value, axis, combine):
    everything = all_in_one(value, axis)
    first = jax.tree.map(lambda part: part[0], everything)

    def turn(k, so_far):
        return combine(so_far, jax.tree.map(lambda part: part[k], everything))

    return lax.fori_loop(1, lax.axis_size(axis), turn, first)


def in_blocks(value, dim, peers):
    before, after = (value.shape[:dim], value.shape[dim + 1 :])
    return jnp.moveaxis(value.reshape(*before, peers, -1, *after), dim, 0)


def summed_on_arrival(value, axis, dim):
    parts = in_blocks(value, dim, lax.axis_size(axis))
    arrived = lax.all_to_all(parts, axis, split_axis=0, concat_axis=0, tiled=True)
    return arrived.sum(axis=0)


def merge_softmax(first, second):
    top = jnp.maximum(first[0], second[0])
    total = first[1] * jnp.exp(first[0] - top) + second[1] * jnp.exp(second[0] - top)
    return (top, total)


def body(features, labels, queries, bank, old_conc, neg_index):
    dp_count = lax.axis_size("dp")
    dp_self = lax.axis_index("dp")
    owned = bank.shape[0]
    feat_rows = features.shape[0]
    capacity = 3 * feat_rows // dp_count
    slot_total = dp_count * capacity
    owners = labels // owned
    local = labels - owners * owned
    table = (owners[:, None] == jnp.arange(dp_count, dtype=jnp.int32)[None, :]).astype(jnp.int32)
    running = jnp.cumsum(table, axis=0)
    ranks = jnp.take_along_axis(running, owners[:, None], axis=1)[:, 0] - 1
    slot_of = owners * capacity + ranks
    send_rows = jnp.zeros((slot_total, features.shape[1]), jnp.bfloat16).at[slot_of].set(features)
    send_ids = jnp.full((slot_total,), owned, jnp.int32).at[slot_of].set(local)
    got_rows = lax.all_to_all(send_rows, "dp", split_axis=0, concat_axis=0, tiled=True)
    got_ids = lax.all_to_all(send_ids, "dp", split_axis=0, concat_axis=0, tiled=True)
    onehot = (jnp.arange(owned, dtype=jnp.int32)[:, None] == got_ids[None, :]).astype(jnp.bfloat16)
    sums = jnp.dot(onehot, got_rows, preferred_element_type=jnp.float32)
    counts = jnp.sum(onehot, axis=1, dtype=jnp.float32)
    touched = counts > 0
    safe_counts = jnp.maximum(counts, 1.0)
    blended = 0.5 * bank + 0.5 * sums / safe_counts[:, None]
    new_bank = jnp.where(touched[:, None], blended, bank)
    valid = got_ids < owned
    safe_ids = jnp.minimum(got_ids, owned - 1)
    differ = got_rows.astype(jnp.float32) - new_bank[safe_ids]
    squared = lax.psum(jnp.sum(differ * differ, axis=1), "mp")
    dist = jnp.where(valid, jnp.sqrt(squared + 0.25), 0.0)
    dist_sums = jax.ops.segment_sum(dist, safe_ids, num_segments=owned)
    new_conc = jnp.where(touched, dist_sums / (safe_counts * jnp.log(safe_counts + 10.0)), old_conc)
    scaled = (new_bank / new_conc[:, None]).astype(jnp.bfloat16)
    returned = lax.all_to_all(scaled[safe_ids], "dp", split_axis=0, concat_axis=0, tiled=True)
    pos_rows = returned[slot_of]
    neg_count = neg_index.shape[0] // dp_count
    wanted = lax.dynamic_slice_in_dim(neg_index, dp_self * neg_count, neg_count) - dp_self * owned
    mine = scaled[wanted]
    own_full = lax.all_to_all(mine, "mp", split_axis=0, concat_axis=1, tiled=True)
    neg_full = lax.all_gather(own_full, "dp", axis=0, tiled=True)
    pos_part = jnp.sum(queries.astype(jnp.float32) * pos_rows.astype(jnp.float32), axis=1)
    query_full = gather_directly(queries, "mp", 1)
    negative = lax.dot_general(
        query_full, neg_full, (((1,), (1,)), ((), ())), preferred_element_type=jnp.float32
    )
    positive = taken_together(pos_part, "mp")
    local_top = jnp.max(negative, axis=1)
    local_total = jnp.sum(jnp.exp(negative - local_top[:, None]), axis=1)
    merged_top, merged_total = combined_all((local_top, local_total), "mp", merge_softmax)
    top = jnp.maximum(merged_top, positive)
    exppos = jnp.exp(positive - top)
    total = merged_total * jnp.exp(merged_top - top) + exppos
    weight = (jnp.exp(negative - top[:, None]) / total[:, None]).astype(jnp.bfloat16)
    grad_terms = jnp.dot(weight, neg_full, preferred_element_type=jnp.float32)
    grad_negs = summed_on_arrival(grad_terms, "mp", 1)
    loss = jnp.log(total) + top - positive
    grad = grad_negs + (exppos / total - 1.0)[:, None] * pos_rows.astype(jnp.float32)
    return (new_bank, new_conc, loss, grad)


def solution(mesh):
    placed = (P("dp", "mp"), P("dp"), P("dp", "mp"), P("dp", "mp"), P("dp"), P())
    return jax.shard_map(
        body,
        mesh=mesh,
        in_specs=placed,
        out_specs=(P("dp", "mp"), P("dp"), P("dp"), P("dp", "mp")),
        check_vma=False,
    )
```

profile of v0, /device:TPU:1, one launch (start us, length us, event | category | flops | bytes accessed | tf_op | source)
XLA Modules:
  0.0 230.0 jit_solution(9466630171139338556)
XLA Ops:
  7.2 0.7 multiply_subtract_fusion
  8.0 0.2 fusion.8
  8.4 2.4 %gather_fusion.4 = s32[256]{0:T(256)S(1)} fusion(s32[256,128]{0,1:T(8,128)S(1)} %bitcast.44, s32[256]{0:T(256)S(1)} %bitcast.43), kind=kCustom, calls=%fused_computation.4 | custom fusion | bytes 4096 | tf_op jit(solution)/shard_map/jit(take_along_axis)/gather | solution.py:83
  10.8 1.4 scatter_custom_fusion
  12.2 0.8 all_to_all.46
  13.0 16.3 %all-to-all-start = ((s32[128,6,1]{1,2,0:T(1,128)}), s32[128,6,1]{1,2,0:T(1,128)S(1)}, u32[]{:S(2)}, u32[]{:S(2)}) async-start(s32[128,6,1]{1,2,0:T(1,128)} %bitcast.7), calls=%async_computation | async-start | bytes 131072 | tf_op jit(solution)/shard_map/all_to_all | solution.py:88
  29.3 2.1 scatter_custom_fusion.1
  31.4 1.1 all_to_all.48
  32.5 7.4 %all-to-all-done = s32[128,6,1]{1,2,0:T(1,128)S(1)} async-done(((s32[128,6,1]{1,2,0:T(1,128)}), s32[128,6,1]{1,2,0:T(1,128)S(1)}, u32[]{:S(2)}, u32[]{:S(2)}) %all-to-all-start) | async-done | bytes 3104 | tf_op jit(solution)/shard_map/all_to_all | solution.py:88
  39.9 6.2 %all-to-all-start.1 = ((bf16[128,6,384]{2,1,0:T(8,128)(2,1)}), bf16[128,6,384]{2,1,0:T(8,128)(2,1)S(1)}, u32[]{:S(2)}, u32[]{:S(2)}) async-start(bf16[128,6,384]{2,1,0:T(8,128)(2,1)} %all_to_all.48), calls=%async_computation.1 | async-start | bytes 1572864 | tf_op jit(solution)/shard_map/all_to_all | solution.py:87
  46.1 0.8 compare_select_fusion.3
  46.9 0.5 broadcast.173
  47.4 1.0 fusion.21
  48.4 0.7 reshape.250
  49.1 0.1 min.22
  49.3 0.1 eq.37
  49.5 0.4 convert_reduce_fusion
  49.9 16.8 %all-to-all-done.1 = bf16[128,6,384]{2,1,0:T(8,128)(2,1)S(1)} async-done(((bf16[128,6,384]{2,1,0:T(8,128)(2,1)}), bf16[128,6,384]{2,1,0:T(8,128)(2,1)S(1)}, u32[]{:S(2)}, u32[]{:S(2)}) %all-to-all-start.1) | async-done | bytes 589856 | tf_op jit(solution)/shard_map/all_to_all | solution.py:87
  66.7 0.2 all_to_all.50
  66.9 2.5 %add_select_fusion = f32[1024,384]{1,0:T(8,128)S(1)} fusion(f32[1024,384]{1,0:T(8,128)} %param.9, bf16[768,384]{1,0:T(8,128)(2,1)S(1)} %all_to_all.50, s32[768]{0:T(1024)S(1)} %eq.37, f32[1024]{0:T(1024)S(1)} %broadcast_maximum_fusion, pred[1024]{0:T(1024)(128)(4,1)S(1)} %broadcast_compare_fusion), kind=kOutput, calls=%fused_computation.17 | convolution fusion | flops 606732288 | bytes 3743744 | tf_op jit(solution)/shard_map/dot_general | solution.py:90
  69.4 2.1 gather_fusion
  71.5 1.3 gather.23
  72.8 1.8 multiply_reduce_fusion
  74.8 6.9 %psum.7 = f32[768]{0:T(1024)S(1)} all-reduce(f32[768]{0:T(1024)S(1)} %reduce_sum.58), channel_id=1, replica_groups=mesh['dp'=128,'mp'=2] {'mp'}, use_global_device_ids=true, to_apply=%region_6.7 | all-reduce | flops 768 | bytes 6144 | tf_op jit(solution)/shard_map/psum | solution.py:99
  81.7 6.0 %scatter_custom_fusion.2 = f32[1024]{0:T(1024)S(1)} fusion(s32[768]{0:T(1024)} %reshape.250, f32[768]{0:T(1024)S(1)} %sqrt_select_fusion, f32[]{:T(128)} %constant.46.clone.1), kind=kCustom, calls=%fused_computation.45 | custom fusion | flops 768 | bytes 4608 | tf_op jit(solution)/shard_map/scatter-add | solution.py:101
  87.7 0.2 divide_convert_fusion.2
  87.9 0.7 gather_fusion.1
  88.6 3.8 %all_to_all.68 = bf16[2,32,384]{2,1,0:T(8,128)(2,1)S(1)} all-to-all(bf16[2,32,384]{2,1,0:T(8,128)(2,1)S(1)} %bitcast.54), channel_id=1, replica_groups=mesh['dp'=128,'mp'=2] {'mp'}, dimensions={0} | all-to-all | bytes 98304 | tf_op jit(solution)/shard_map/all_to_all | solution.py:109
  92.4 0.6 copy.39
  93.0 2.6 %gather_fusion.2 = bf16[768,384]{1,0:T(8,128)(2,1)S(1)} fusion(bf16[1024,384]{1,0:T(8,128)(2,1)S(1)} %divide_convert_fusion.2, s32[1024]{0:T(1024)S(1)} %pad_clamp_fusion.2), kind=kCustom, calls=%fused_computation.2 | custom fusion | bytes 1182720 | tf_op jit(solution)/shard_map/gather | solution.py:104
  95.7 1.1 all_to_all.56
  96.8 7.0 %all-to-all-start.4 = ((bf16[128,6,384]{2,1,0:T(8,128)(2,1)}), bf16[128,6,384]{2,1,0:T(8,128)(2,1)S(1)}, u32[]{:S(2)}, u32[]{:S(2)}) async-start(bf16[128,6,384]{2,1,0:T(8,128)(2,1)} %all_to_all.56), calls=%async_computation.4 | async-start | bytes 1572864 | tf_op jit(solution)/shard_map/all_to_all | solution.py:104
  103.8 0.1 copy.34
  104.0 22.9 %all-to-all-done.4 = bf16[128,6,384]{2,1,0:T(8,128)(2,1)S(1)} async-done(((bf16[128,6,384]{2,1,0:T(8,128)(2,1)}), bf16[128,6,384]{2,1,0:T(8,128)(2,1)S(1)}, u32[]{:S(2)}, u32[]{:S(2)}) %all-to-all-start.4) | async-done | bytes 589856 | tf_op jit(solution)/shard_map/all_to_all | solution.py:104
  126.9 0.2 all_to_all.58
  127.1 1.2 gather_fusion.3
  128.4 6.6 %all_to_all.69 = f32[2,1,256]{2,1,0:T(1,128)S(1)} all-to-all(f32[2,1,256]{2,1,0:T(1,128)S(1)} %broadcast_in_dim.55), channel_id=1, replica_groups=mesh['dp'=128,'mp'=2] {'mp'}, dimensions={0} | all-to-all | bytes 4096 | tf_op jit(solution)/shard_map/all_to_all | solution.py:9
  135.0 0.8 broadcast_in_dim.54
  135.8 3.8 %all-to-all-start.3 = ((bf16[2,256,384]{1,2,0:T(8,128)(2,1)}), bf16[2,256,384]{1,2,0:T(8,128)(2,1)S(1)}, u32[]{:S(2)}, u32[]{:S(2)}) async-start(bf16[2,256,384]{1,2,0:T(8,128)(2,1)} %broadcast_in_dim.54), calls=%async_computation.3 | async-start | bytes 786432 | tf_op jit(solution)/shard_map/all_to_all | solution.py:9
  139.6 1.3 all-to-all-done.3
  140.8 63.3 %all-gather.4.cloned.1.call-done = bf16[4096,768]{1,0:T(8,128)(2,1)} async-done(((bf16[32,768]{1,0:T(8,128)(2,1)}), bf16[4096,768]{1,0:T(8,128)(2,1)}) %all-gather.4.cloned.1.call-update) | async-done | bytes 6291472 | tf_op jit(solution)/shard_map/all_gather | solution.py:110
  204.2 4.8 %fusion.23 = (f32[256]{0:T(256)S(1)}, f32[4096,256]{1,0:T(8,128)S(1)}) fusion(bf16[4096,768]{1,0:T(8,128)(2,1)} %all-gather.4.cloned.1.call-done, bf16[256,768]{0,1:T(8,128)(2,1)S(1)} %bitcast.46), kind=kOutput, calls=%fused_computation.70 | convolution fusion | flops 1611661056 | bytes 10880000 | tf_op jit(solution)/shard_map/dot_general | solution.py:113
  209.0 0.6 exponential_reduce_fusion
  209.7 5.7 %all-gather.1 = f32[2,2,256]{2,1,0:T(2,128)S(1)} all-gather(f32[1,2,256]{2,1,0:T(2,128)S(1)} %maximum_bitcast_fusion), channel_id=2, replica_groups=mesh['dp'=128,'mp'=2] {'mp'}, dimensions={0}, use_global_device_ids=true | all-gather | bytes 6144 | tf_op jit(solution)/shard_map/all_gather | solution.py:36
  215.4 0.6 add_subtract_fusion
  216.0 1.9 fusion.2
  217.9 4.3 %all_to_all.70 = f32[2,256,384]{2,1,0:T(8,128)S(1)} all-to-all(f32[2,256,384]{2,1,0:T(8,128)S(1)} %bitcast.45), channel_id=1, replica_groups=mesh['dp'=128,'mp'=2] {'mp'}, dimensions={0} | all-to-all | bytes 1572864 | tf_op jit(solution)/shard_map/all_to_all | solution.py:62
  222.3 0.9 fusion.5
  (46 shorter events, 0.9 us)
Async XLA Ops:
  10.8 29.1 %copy-start.4 = (s32[256]{0:T(256)}, s32[256]{0:T(256)S(1)}, u32[]{:S(2)}) copy-start(s32[256]{0:T(256)S(1)} %compare_select_fusion.1) | copy-start | bytes 3076
  13.0 26.9 %all-to-all-start = ((s32[128,6,1]{1,2,0:T(1,128)}), s32[128,6,1]{1,2,0:T(1,128)S(1)}, u32[]{:S(2)}, u32[]{:S(2)}) async-start(s32[128,6,1]{1,2,0:T(1,128)} %bitcast.7), calls=%async_computation | async-start | bytes 131072 | tf_op jit(solution)/shard_map/all_to_all | solution.py:88
  39.9 26.8 %all-to-all-start.1 = ((bf16[128,6,384]{2,1,0:T(8,128)(2,1)}), bf16[128,6,384]{2,1,0:T(8,128)(2,1)S(1)}, u32[]{:S(2)}, u32[]{:S(2)}) async-start(bf16[128,6,384]{2,1,0:T(8,128)(2,1)} %all_to_all.48), calls=%async_computation.1 | async-start | bytes 1572864 | tf_op jit(solution)/shard_map/all_to_all | solution.py:87
  46.1 158.1 %all-gather.4.cloned.1.call-start = ((), (), s32[]{:S(2)}) async-start(), calls=%async_computation.7 | async-start | bytes 6340608 | tf_op jit(solution)/shard_map/all_gather | solution.py:110
  69.4 18.3 %copy-start = (f32[1024,384]{1,0:T(8,128)}, f32[1024,384]{1,0:T(8,128)S(1)}, u32[]{:S(2)}) copy-start(f32[1024,384]{1,0:T(8,128)S(1)} %add_select_fusion) | copy-start | bytes 4718596
  72.8 14.8 %copy-start.6 = (f32[1024]{0:T(1024)S(1)}, f32[1024]{0:T(1024)}, u32[]{:S(2)}) copy-start(f32[1024]{0:T(1024)} %param.10) | copy-start | bytes 12292
  87.7 8.0 %copy-start.3 = (f32[1024]{0:T(1024)}, f32[1024]{0:T(1024)S(1)}, u32[]{:S(2)}) copy-start(f32[1024]{0:T(1024)S(1)} %divide_select_fusion) | copy-start | bytes 12292
  95.7 8.1 %copy-start.2 = (bf16[256,384]{1,0:T(8,128)(2,1)S(1)}, bf16[256,384]{1,0:T(8,128)(2,1)}, u32[]{:S(2)}) copy-start(bf16[256,384]{1,0:T(8,128)(2,1)} %param.8) | copy-start | bytes 589828
  95.7 8.3 %copy-start.5 = (s32[256]{0:T(256)S(1)}, s32[256]{0:T(256)}, u32[]{:S(2)}) copy-start(s32[256]{0:T(256)} %copy-done.4) | copy-start | bytes 3076
  96.8 30.1 %all-to-all-start.4 = ((bf16[128,6,384]{2,1,0:T(8,128)(2,1)}), bf16[128,6,384]{2,1,0:T(8,128)(2,1)S(1)}, u32[]{:S(2)}, u32[]{:S(2)}) async-start(bf16[128,6,384]{2,1,0:T(8,128)(2,1)} %all_to_all.56), calls=%async_computation.4 | async-start | bytes 1572864 | tf_op jit(solution)/shard_map/all_to_all | solution.py:104
  135.8 5.1 %all-to-all-start.3 = ((bf16[2,256,384]{1,2,0:T(8,128)(2,1)}), bf16[2,256,384]{1,2,0:T(8,128)(2,1)S(1)}, u32[]{:S(2)}, u32[]{:S(2)}) async-start(bf16[2,256,384]{1,2,0:T(8,128)(2,1)} %broadcast_in_dim.54), calls=%async_computation.3 | async-start | bytes 786432 | tf_op jit(solution)/shard_map/all_to_all | solution.py:9
  204.2 11.8 %copy-start.1 = (bf16[4096,768]{1,0:T(8,128)(2,1)S(1)}, bf16[4096,768]{1,0:T(8,128)(2,1)}, u32[]{:S(2)}) copy-start(bf16[4096,768]{1,0:T(8,128)(2,1)} %all-gather.4.cloned.1.call-done) | copy-start | bytes 18874372
Sparse Core Ops, SparseCore 0:
  93.2 110.9 all-gather.3
where the time goes:
time: 231 us; the launch traced here: 230 us
  waiting for transfers between devices  112 us (48%)
  starting transfers between devices  33.4 us (14%)
  blocking collectives  27.3 us (12%)
  local copies, waits for them, and re-layouts  20.6 us (9%)
  between operations  14.4 us (6%)
  other arithmetic  13.5 us (6%)
  matrix products  9.18 us (4%)
    all_gather x1, waiting for transfers between devices, body(): neg_full = lax.all_gather(own_full, 'dp', axis=0, tiled=True)  63.3 us
    all_to_all x1, waiting for transfers between devices, body(): lax.all_to_all(scaled[safe_ids], 'dp', split_axis=0, concat_axis=0, tiled...  22.9 us
    all_to_all x1, waiting for transfers between devices, body(): lax.all_to_all(send_rows, 'dp', split_axis=0, concat_axis=0, tiled=True)  16.8 us
    all_to_all x1, starting transfers between devices, body(): lax.all_to_all(send_ids, 'dp', split_axis=0, concat_axis=0, tiled=True)  16.3 us
    all_to_all x1, waiting for transfers between devices, body(): lax.all_to_all(send_ids, 'dp', split_axis=0, concat_axis=0, tiled=True)  7.37 us
    all_to_all x1, starting transfers between devices, body(): lax.all_to_all(scaled[safe_ids], 'dp', split_axis=0, concat_axis=0, tiled...  7.01 us
    psum x1, blocking collectives, body(): squared = lax.psum(jnp.sum(differ * differ, axis=1), 'mp')  6.91 us
    all_to_all x1, blocking collectives, sent_to_all(): return lax.all_to_all(copies, axis, split_axis=0, concat_axis=0, tiled=True)  6.56 us
  transfers between devices with their start and end apart: 5, of which 5 were waited for; matrix products, arithmetic and copies ran while one was open for 5% of the time, Pallas kernels for 0%

commit v1 on v0

v1 whole, which is shorter than its diff:
```python
import functools
import jax
import jax.numpy as jnp
from jax import lax
from jax.experimental import pallas as pl
from jax.experimental.pallas import tpu as pltpu
from jax.sharding import PartitionSpec as P

MESH = pl.DeviceIdType.MESH
F32, BF16 = jnp.float32, jnp.bfloat16
LEN = {"x": 4, "y": 4, "z": 8}
CHIPS = 128
OWNED = 1024
ROWS = 256
HALF = 384
CAP = 6
TILE = 256


def iota(shape, dim):
    return lax.broadcasted_iota(jnp.int32, shape, dim)


def peer(me, d):
    return lax.rem(me + d, CHIPS)


def blocks_start(src, dst, to, ssem, rsem, lo, hi, me):
    def go(d, _):
        o = peer(me, d)
        pltpu.make_async_remote_copy(
            src(o), dst(me), ssem, rsem, device_id={"dp": o}, device_id_type=MESH
        ).start()
        return 0

    lax.fori_loop(lo, hi, go, 0)


def wait_send(ref, ssem, rsem):
    pltpu.make_async_remote_copy(
        ref, ref, ssem, rsem, device_id={"dp": 0}, device_id_type=MESH
    ).wait_send()


def wait_recv(ref, ssem, rsem):
    pltpu.make_async_remote_copy(
        ref, ref, ssem, rsem, device_id={"dp": 0}, device_id_type=MESH
    ).wait_recv()


def make_colour(own, gathered, ssem, rsem, at_chip, pending, count):
    def chip(axis, v):
        d = dict(at_chip)
        d[axis] = v
        return (d["y"] * 8 + d["z"]) * 4 + d["x"]

    def off(axis, k):
        return lax.rem(at_chip[axis] + k + LEN[axis], LEN[axis])

    def send(src, dst, to):
        i = count[0]
        count[0] += 1
        copy = pltpu.make_async_remote_copy(
            src, dst, ssem.at[i], rsem.at[i], device_id={"dp": to}, device_id_type=MESH
        )
        copy.start()
        pending.append(copy.wait_send)
        return i

    def arrived(ref, i):
        wait_recv(ref, ssem.at[i], rsem.at[i])

    def colour(order, unit, halves):
        a1, a2, a3 = order
        buffer = gathered[unit]
        layout = "xyz" if unit else "zxy"

        def at(k1, k2, k3, part=None):
            pos = {a1: k1, a2: k2, a3: k3}
            idx = []
            for a in layout:
                n = LEN[a]
                if pos[a] is not None:
                    idx.append(pos[a])
                elif part is None:
                    idx.append(pl.ds(0, n))
                else:
                    idx.append(pl.ds(part * (n // 2), n // 2))
            return buffer.at[tuple(idx) + (halves,)]

        mine = own.at[unit, halves]
        c1, c2, c3 = (at_chip[a] for a in order)
        first = [
            (d, send(mine, at(c1, c2, c3), chip(a1, off(a1, d))))
            for d in range(1, LEN[a1])
        ]
        i = count[0]
        count[0] += 1
        local = pltpu.make_async_copy(mine, at(c1, c2, c3), ssem.at[i])
        local.start()
        yield
        local.wait()
        for d, i in first:
            arrived(at(off(a1, -d), c2, c3), i)
        right2, left2 = chip(a2, off(a2, 1)), chip(a2, off(a2, -1))
        right3, left3 = chip(a3, off(a3, 1)), chip(a3, off(a3, -1))
        last = LEN[a3] // 2
        flying = {}

        def start(k2):
            block = at(None, off(a2, k2), c3)
            flying[k2] = (send(block, block, right3), send(block, block, left3))

        def step(k2, s):
            there = off(a2, k2)
            from_left, from_right = flying[k2]
            part = (0, 1) if s == last else (None, None)
            on = (0, 1) if s + 1 == last else (None, None)
            arrived(at(None, there, off(a3, -s), part[0]), from_left)
            if s < last:
                block = at(None, there, off(a3, -s), on[0])
                i = send(block, block, right3)
            arrived(at(None, there, off(a3, s), part[1]), from_right)
            if s < last:
                block = at(None, there, off(a3, s), on[1])
                flying[k2] = (i, send(block, block, left3))

        block = at(None, c2, c3)
        to_r, to_l = send(block, block, right2), send(block, block, left2)
        start(0)
        yield
        arrived(at(None, off(a2, -1), c3), to_r)
        arrived(at(None, off(a2, 1), c3), to_l)
        block = at(None, off(a2, -1), c3, 0)
        to_r = send(block, block, right2)
        block = at(None, off(a2, 1), c3, 1)
        to_l = send(block, block, left2)
        start(-1)
        start(1)
        yield
        arrived(at(None, off(a2, 2), c3, 0), to_r)
        arrived(at(None, off(a2, 2), c3, 1), to_l)
        start(2)
        yield
        for s in range(1, last + 1):
            for k2 in (0, -1, 1, 2):
                step(k2, s)
            yield

    return colour


def as_column(row, n):
    eye = iota((n, n), 0) == iota((n, n), 1)
    return jnp.sum(jnp.where(eye, row, jnp.zeros_like(row)), axis=1, keepdims=True)


def kernel(
    feat, labels, q, bank, old_conc, negs,
    new_bank, new_conc, loss, grad,
    sent, sent_ids, got, got_ids, back, returned, route, wide,
    d2_mine, d2_theirs, nb16, scaled, count_of, conc_of, mine, own,
    g0, g1, g2, g3, qf, acc, stats, acc_in, stats_in,
    ag_send, ag_recv, sem,
):
    me = lax.axis_index("dp")
    core = lax.axis_index("mp")
    other = 1 - core
    at_chip = {
        "x": lax.rem(me, 4),
        "y": lax.div(me, 32),
        "z": lax.rem(lax.div(me, 4), 8),
    }

    def to_partner(src, dst, k):
        return pltpu.make_async_remote_copy(
            src, dst, sem.at[k], sem.at[k + 1], device_id={"mp": other}, device_id_type=MESH
        )

    def clear(k, _):
        rows = pl.ds(k * 16, 16)
        got[rows, :, 0:HALF] = jnp.zeros((16, 8, HALF), BF16)
        got[rows, :, HALF:] = jnp.ones((16, 8, 128), BF16)
        returned[rows] = jnp.zeros((16, 8, HALF), BF16)
        return 0

    lax.fori_loop(0, CHIPS // 16, clear, 0)

    barrier = pltpu.get_barrier_semaphore()

    def greet(d, _):
        pl.semaphore_signal(
            barrier, inc=1, device_id={"dp": peer(me, d)}, device_id_type=MESH
        )
        return 0

    lax.fori_loop(1, CHIPS, greet, 0)
    pl.semaphore_signal(barrier, inc=1, device_id={"mp": other}, device_id_type=MESH)

    lab_row = labels[...]
    own_row = lax.shift_right_logical(lab_row, 10)
    own_col = as_column(own_row.astype(F32), ROWS).astype(jnp.int32)
    same = own_col == own_row
    r_i, c_i = iota((ROWS, ROWS), 0), iota((ROWS, ROWS), 1)
    rank_row = jnp.sum(jnp.where(same & (r_i < c_i), 1.0, 0.0), axis=0, keepdims=True)
    rank_col = jnp.sum(jnp.where(same & (c_i < r_i), 1.0, 0.0), axis=1, keepdims=True)
    slot_row = own_row * 8 + rank_row.astype(jnp.int32)
    slot_col = own_col * 8 + rank_col.astype(jnp.int32)
    lab_col = as_column(lab_row.astype(F32), ROWS).astype(jnp.int32)
    id_col = jnp.bitwise_and(lab_col, OWNED - 1) + 1
    at_rank = iota((ROWS, 128), 1) == rank_col.astype(jnp.int32)
    hi = jnp.where(at_rank, lax.shift_right_logical(id_col, 5).astype(F32), 0.0).astype(BF16)
    lo = jnp.where(at_rank, jnp.bitwise_and(id_col, 31).astype(F32), 0.0).astype(BF16)
    fv = feat[...]
    for k in range(OWNED // TILE):
        r = iota((TILE, ROWS), 0) + k * TILE
        pick = jnp.where(r == slot_row, 1.0, 0.0).astype(BF16)
        rows = jnp.dot(pick, fv, preferred_element_type=F32).astype(BF16)
        sent[k * 32 : (k + 1) * 32] = rows.reshape(32, 8, HALF)
        pick = jnp.where(r == own_row * 8, 1.0, 0.0).astype(BF16)
        ids = jnp.dot(pick, hi, preferred_element_type=F32) * 32.0
        ids = ids + jnp.dot(pick, lo, preferred_element_type=F32)
        sent_ids[k * 32 : (k + 1) * 32] = ids.reshape(32, 8, 128)
    c = iota((ROWS, OWNED), 1)
    route[...] = jnp.where(c == slot_col, 1.0, 0.0).astype(BF16)

    pl.semaphore_wait(barrier, CHIPS)

    six = pl.ds(0, CAP)
    left = pl.ds(0, HALF)
    blocks_start(
        lambda o: sent_ids.at[o, pl.ds(0, 1)], lambda o: got_ids.at[o, pl.ds(0, 1)],
        None, sem.at[0], sem.at[1], 1, CHIPS, me,
    )
    blocks_start(
        lambda o: sent.at[o, six], lambda o: got.at[o, six, left],
        None, sem.at[2], sem.at[3], 1, CHIPS, me,
    )
    qx = to_partner(q, qf.at[core], 8)
    qx.start()
    home = [
        pltpu.make_async_copy(sent_ids.at[me, pl.ds(0, 1)], got_ids.at[me, pl.ds(0, 1)], sem.at[10]),
        pltpu.make_async_copy(sent.at[me, six], got.at[me, six, left], sem.at[11]),
        pltpu.make_async_copy(q, qf.at[core], sem.at[12]),
    ]
    for copy in home:
        copy.start()
    for copy in home:
        copy.wait()
    rest = pl.ds(0, CHIPS - 1)
    wait_recv(got_ids.at[rest, pl.ds(0, 1)], sem.at[0], sem.at[1])

    spread = jnp.broadcast_to(got_ids[:, 0:1, :], (CHIPS, 8, 128))
    here = iota((CHIPS, 8, 128), 1) == iota((CHIPS, 8, 128), 2)
    id_c = jnp.sum(jnp.where(here, spread, 0.0), axis=2, keepdims=True) - 1.0
    wide[...] = jnp.broadcast_to(id_c, (CHIPS, 8, 128)).reshape(OWNED, 128)
    id_row = jnp.transpose(wide[...])[0:1, :].astype(jnp.int32)
    wait_recv(got.at[rest, six, left], sem.at[2], sem.at[3])

    gv = got[...].reshape(OWNED, HALF + 128)
    for k in range(OWNED // TILE):
        rows = pl.ds(k * TILE, TILE)
        hit = jnp.where(iota((TILE, OWNED), 0) + k * TILE == id_row, 1.0, 0.0).astype(BF16)
        sums = jnp.dot(hit, gv, preferred_element_type=F32)
        counts = sums[:, HALF : HALF + 1]
        old = bank[rows, :]
        mixed = 0.5 * old + 0.5 * sums[:, 0:HALF] / jnp.maximum(counts, 1.0)
        fresh = jnp.where(counts > 0, mixed, old)
        new_bank[rows, :] = fresh
        nb16[rows, :] = fresh.astype(BF16)
        count_of[rows, :] = sums[:, HALF:]

    nbv = nb16[...]
    for k in range(OWNED // TILE):
        rows = pl.ds(k * TILE, TILE)
        ids = wide[rows, :][:, 0:1].astype(jnp.int32)
        hit = jnp.where(iota((TILE, OWNED), 1) == ids, 1.0, 0.0).astype(BF16)
        near = jnp.dot(hit, nbv, preferred_element_type=F32)
        apart = got[k * 32 : (k + 1) * 32, :, 0:HALF].reshape(TILE, HALF).astype(F32) - near
        d2 = jnp.sum(apart * apart, axis=1, keepdims=True)
        d2_mine[:, k * TILE : (k + 1) * TILE] = jnp.transpose(jnp.broadcast_to(d2, (TILE, 128)))[0:8, :]
    d2x = to_partner(d2_mine, d2_theirs, 13)
    d2x.start()
    neg_row = negs[pl.ds(lax.div(me, 2), 1), :]
    want = as_column(neg_row.astype(F32), 128).astype(jnp.int32) - me * OWNED
    old_col = jnp.transpose(jnp.broadcast_to(old_conc[...], (128, OWNED)))
    conc_of[...] = old_col
    d2x.wait()

    dist = jnp.sqrt(d2_mine[0:1, :] + d2_theirs[0:1, :] + 0.25)
    for k in range(OWNED // TILE):
        rows = pl.ds(k * TILE, TILE)
        on = iota((TILE, OWNED), 0) + k * TILE == id_row
        total = jnp.sum(jnp.where(on, dist, 0.0), axis=1, keepdims=True)
        counts = count_of[rows, :][:, 0:1]
        safe = jnp.maximum(counts, 1.0)
        conc = jnp.where(counts > 0, total / (safe * jnp.log(safe + 10.0)), conc_of[rows, :][:, 0:1])
        scaled[rows, :] = (new_bank[rows, :] / conc).astype(BF16)
        conc_of[rows, :] = jnp.broadcast_to(conc, (TILE, 128))

    sv = scaled[...]
    hit = jnp.where(iota((128, OWNED), 1) == want, 1.0, 0.0).astype(BF16)
    mine[...] = jnp.dot(hit, sv, preferred_element_type=F32).astype(BF16).reshape(16, 8, HALF)
    base = lax.rem(me, 2) * 8
    mx = to_partner(mine.at[pl.ds(base + other * 4, 4)], own.at[:, core], 15)
    mx.start()
    keep = pltpu.make_async_copy(mine.at[pl.ds(base + core * 4, 4)], own.at[:, core], sem.at[17])
    keep.start()
    keep.wait()
    new_conc[...] = jnp.transpose(conc_of[...])[0:1, :]
    mx.wait()

    pending = []
    count = [0]
    colour = make_colour(own, (g0, g1, g2, g3), ag_send, ag_recv, at_chip, pending, count)
    both = pl.ds(0, 2)
    live = [
        colour("yxz", 0, both),
        colour("zyx", 1, both),
        colour("zxy", 2, both),
        colour("zyx", 3, pl.ds(0, 1)),
        colour("zxy", 3, pl.ds(1, 1)),
    ]

    def advance():
        for g in list(live):
            try:
                next(g)
            except StopIteration:
                live.remove(g)

    advance()

    for k in range(OWNED // TILE):
        rows = pl.ds(k * TILE, TILE)
        ids = wide[rows, :][:, 0:1].astype(jnp.int32)
        hit = jnp.where(iota((TILE, OWNED), 1) == ids, 1.0, 0.0).astype(BF16)
        out = jnp.dot(hit, sv, preferred_element_type=F32).astype(BF16)
        back[k * 32 : (k + 1) * 32] = out.reshape(32, 8, HALF)
    advance()
    blocks_start(
        lambda o: back.at[o, six], lambda o: returned.at[o, six],
        None, sem.at[4], sem.at[5], 1, CHIPS, me,
    )
    copy = pltpu.make_async_copy(back.at[me, six], returned.at[me, six], sem.at[18])
    copy.start()
    copy.wait()
    qx.wait()
    stats[...] = jnp.full((ROWS, 128), -3.0e38, F32)
    acc[...] = jnp.zeros((2, ROWS, HALF), F32)
    while live:
        advance()

    q0, q1 = qf[0], qf[1]
    top = jnp.full((ROWS, 1), -3.0e38, F32)
    sums = jnp.zeros((ROWS, 1), F32)
    nt = (((1,), (1,)), ((), ()))
    for g in (g0, g1, g2, g3):
        if g is g0:
            plan = [(pl.ds(2 * k, 2),) for k in range(4)]
        else:
            plan = [(pl.ds(k, 1),) for k in range(4)]

        for (part,) in plan:
            k0 = g[part, :, :, 0].reshape(TILE, HALF)
            k1 = g[part, :, :, 1].reshape(TILE, HALF)
            s = lax.dot_general(q0, k0, nt, preferred_element_type=F32)
            s = s + lax.dot_general(q1, k1, nt, preferred_element_type=F32)
            higher = jnp.maximum(top, jnp.max(s, axis=1, keepdims=True))
            shrink = jnp.exp(top - higher)
            p = jnp.exp(s - higher)
            sums = sums * shrink + jnp.sum(p, axis=1, keepdims=True)
            pb = p.astype(BF16)
            acc[0] = acc[0] * shrink + jnp.dot(pb, k0, preferred_element_type=F32)
            acc[1] = acc[1] * shrink + jnp.dot(pb, k1, preferred_element_type=F32)
            top = higher

    wait_recv(returned.at[rest, six], sem.at[4], sem.at[5])
    pos_rows = jnp.dot(
        route[...], returned[...].reshape(OWNED, HALF), preferred_element_type=F32
    )
    part = jnp.sum(q[...].astype(F32) * pos_rows, axis=1, keepdims=True)
    lane = iota((ROWS, 128), 1)
    stats[...] = jnp.where(lane == 0, top, jnp.where(lane == 1, sums, part))
    ax = to_partner(acc.at[other], acc_in, 19)
    sx = to_partner(stats, stats_in, 21)
    ax.start()
    sx.start()
    ax.wait()
    sx.wait()
    t2, s2, p2 = stats_in[:, 0:1], stats_in[:, 1:2], stats_in[:, 2:3]
    positive = part + p2
    peak = jnp.maximum(jnp.maximum(top, t2), positive)
    w1, w2, wp = jnp.exp(top - peak), jnp.exp(t2 - peak), jnp.exp(positive - peak)
    total = sums * w1 + s2 * w2 + wp
    lcol = jnp.log(total) + peak - positive
    loss[...] = jnp.transpose(jnp.broadcast_to(lcol, (ROWS, 128)))[0:1, :]
    grad[...] = (
        (acc[core] * w1 + acc_in[...] * w2) / total + (wp / total - 1.0) * pos_rows
    )

    for wait in pending:
        wait()
    wait_send(sent_ids.at[rest, pl.ds(0, 1)], sem.at[0], sem.at[1])
    wait_send(sent.at[rest, six], sem.at[2], sem.at[3])
    wait_send(back.at[rest, six], sem.at[4], sem.at[5])


def body(features, labels, queries, bank, old_conc, neg_index):
    vmem = pl.BlockSpec(memory_space=pltpu.VMEM)
    big = (4, 4, 8, 2, 8, HALF)
    outs = pl.pallas_call(
        kernel,
        out_shape=(
            jax.ShapeDtypeStruct((OWNED, HALF), F32),
            jax.ShapeDtypeStruct((1, OWNED), F32),
            jax.ShapeDtypeStruct((1, ROWS), F32),
            jax.ShapeDtypeStruct((ROWS, HALF), F32),
        ),
        in_specs=[vmem] * 6,
        out_specs=(vmem,) * 4,
        scratch_shapes=[
            pltpu.VMEM((CHIPS, 8, HALF), BF16),
            pltpu.VMEM((CHIPS, 8, 128), F32),
            pltpu.VMEM((CHIPS, 8, HALF + 128), BF16),
            pltpu.VMEM((CHIPS, 8, 128), F32),
            pltpu.VMEM((CHIPS, 8, HALF), BF16),
            pltpu.VMEM((CHIPS, 8, HALF), BF16),
            pltpu.VMEM((ROWS, OWNED), BF16),
            pltpu.VMEM((OWNED, 128), F32),
            pltpu.VMEM((8, OWNED), F32),
            pltpu.VMEM((8, OWNED), F32),
            pltpu.VMEM((OWNED, HALF), BF16),
            pltpu.VMEM((OWNED, HALF), BF16),
            pltpu.VMEM((OWNED, 128), F32),
            pltpu.VMEM((OWNED, 128), F32),
            pltpu.VMEM((16, 8, HALF), BF16),
            pltpu.VMEM((4, 2, 8, HALF), BF16),
            pltpu.VMEM((8, 4, 4, 2, 8, HALF), BF16),
            pltpu.VMEM(big, BF16),
            pltpu.VMEM(big, BF16),
            pltpu.VMEM(big, BF16),
            pltpu.VMEM((2, ROWS, HALF), BF16),
            pltpu.VMEM((2, ROWS, HALF), F32),
            pltpu.VMEM((ROWS, 128), F32),
            pltpu.VMEM((ROWS, HALF), F32),
            pltpu.VMEM((ROWS, 128), F32),
            pltpu.SemaphoreType.DMA((160,)),
            pltpu.SemaphoreType.DMA((160,)),
            pltpu.SemaphoreType.DMA((24,)),
        ],
        compiler_params=pltpu.CompilerParams(
            collective_id=0, has_side_effects=True, vmem_limit_bytes=60 << 20
        ),
        name="step",
    )(
        features,
        labels.reshape(1, ROWS),
        queries,
        bank,
        old_conc.reshape(1, OWNED),
        neg_index.reshape(64, 128),
    )
    new_bank, new_conc, loss, grad = outs
    return new_bank, new_conc.reshape(OWNED), loss.reshape(ROWS), grad


def solution(mesh):
    return jax.shard_map(
        body,
        mesh=mesh,
        in_specs=(P("dp", "mp"), P("dp"), P("dp", "mp"), P("dp", "mp"), P("dp"), P()),
        out_specs=(P("dp", "mp"), P("dp"), P("dp"), P("dp", "mp")),
        check_vma=False,
    )
```

time: 231 us -> 103 us (0.45)
  waiting for transfers between devices: 112 us -> 0 us
  Pallas kernels: 0 us -> 97.5 us
  starting transfers between devices: 33.4 us -> 0 us
  blocking collectives: 27.3 us -> 0 us
  local copies, waits for them, and re-layouts: 20.6 us -> 4.62 us
  between operations: 14.4 us -> 0.67 us
  other arithmetic: 13.5 us -> 0 us
  matrix products: 9.18 us -> 0 us
    pallas_call x0 -> x1, Pallas kernels: none -> 97.5 us  [body(): pl.pallas_call(kernel, out_shape=(jax.ShapeDtypeStruct((OWNED, HALF), F32...]
    all_gather x1 -> x0, waiting for transfers between devices: 63.3 us -> none  [body(): neg_full = lax.all_gather(own_full, 'dp', axis=0, tiled=True)]
    all_to_all x4 -> x0, waiting for transfers between devices: 48.4 us -> none  [the longest x1 22.9 us: body(): lax.all_to_all(scaled[safe_ids], 'dp', split_axis=0, concat_axis=0, tiled...]
    all_to_all x4 -> x0, starting transfers between devices: 33.3 us -> none  [the longest x1 16.3 us: body(): lax.all_to_all(send_ids, 'dp', split_axis=0, concat_axis=0, tiled=True)]
    all_to_all x3 -> x0, blocking collectives: 14.7 us -> none  [the longest x1 6.56 us: sent_to_all(): return lax.all_to_all(copies, axis, split_axis=0, concat_axis=0, tiled=True)]
    gather x6 -> x0, local copies, waits for them, and re-layouts: 10.3 us -> none  [the longest x2 3.44 us: body(): differ = got_rows.astype(jnp.float32) - new_bank[safe_ids]]
    dot_general x3 -> x0, matrix products: 9.18 us -> none  [the longest x1 4.83 us: body(): lax.dot_general(query_full, neg_full, (((1,), (1,)), ((), ())), preferred...]
    psum x1 -> x0, blocking collectives: 6.91 us -> none  [body(): squared = lax.psum(jnp.sum(differ * differ, axis=1), 'mp')]
  transfers between devices with their start and end apart: 5 -> 0, of which waited for: 5 -> 0; matrix products, arithmetic and copies ran while one was open for 5% -> 0% of each run, Pallas kernels for 0% -> 0%
where the time goes in v1:
time: 103 us
  Pallas kernels  97.5 us (95%)
  local copies, waits for them, and re-layouts  4.62 us (4%)
    pallas_call x1, Pallas kernels, body(): pl.pallas_call(kernel, out_shape=(jax.ShapeDtypeStruct((OWNED, HALF), F32...  97.5 us
    unnamed x10, local copies, waits for them, and re-layouts  4.62 us

profile of v1, /device:TPU:1, one launch (start us, length us, event | category | flops | bytes accessed | tf_op | source)
XLA Modules:
  0.0 102.7 jit_solution(5823848690734865280)
XLA Ops:
  0.6 97.5 %step.1 = (f32[1024,384]{1,0:T(8,128)}, f32[1,1024]{1,0:T(1,128)}, f32[1,256]{1,0:T(1,128)}, f32[256,384]{1,0:T(8,128)}) custom-call(bf16[256,384]{1,0:T(8,128)(2,1)} %feat.1, s32[1,256]{1,0:T(1,128)} %bitcast.8, bf16[256,384]{1,0:T(8,128)(2,1)} %q.1, f32[1024,384]{1,0:T(8,128)} %bank.1, f32[1,1024]{1,0:T(1,128)} %bitcast.6, s32[64,128]{1,0:T(8,128)} %bitcast.5), custom_call_target="tpu_custom_call" | custom-call | tf_op jit(solution)/shard_map/step/pallas_call | solution.py:412
  98.1 0.0 copy-start.1
  98.1 0.0 copy-start.2
  98.1 0.0 copy-start
  98.1 2.7 %copy.14 = f32[1024,384]{1,0:T(8,128)} copy(f32[1024,384]{1,0:T(8,128)} %get-tuple-element.16) | data formatting | bytes 3145728
  100.8 0.0 copy-done.1
  100.8 0.6 copy.15
  101.4 0.0 copy-done.2
  101.4 0.6 copy.16
  102.0 0.0 copy-done
  102.0 0.7 copy.17
Async XLA Ops:
  98.1 2.7 %copy-start.1 = (f32[1,1024]{1,0:T(1,128)S(1)}, f32[1,1024]{1,0:T(1,128)}, u32[]{:S(2)}) copy-start(f32[1,1024]{1,0:T(1,128)} %get-tuple-element.9) | copy-start | bytes 12292
  98.1 3.3 %copy-start.2 = (f32[1,256]{1,0:T(1,128)S(1)}, f32[1,256]{1,0:T(1,128)}, u32[]{:S(2)}) copy-start(f32[1,256]{1,0:T(1,128)} %get-tuple-element.10) | copy-start | bytes 3076
  98.1 3.9 %copy-start = (f32[256,384]{1,0:T(8,128)S(1)}, f32[256,384]{1,0:T(8,128)}, u32[]{:S(2)}) copy-start(f32[256,384]{1,0:T(8,128)} %get-tuple-element.19) | copy-start | bytes 1179652

commit v2 on v1

v2 whole, which is shorter than its diff:
```python
import functools
import jax
import jax.numpy as jnp
from jax import lax
from jax.experimental import pallas as pl
from jax.experimental.pallas import tpu as pltpu
from jax.sharding import PartitionSpec as P

MESH = pl.DeviceIdType.MESH
F32, BF16 = jnp.float32, jnp.bfloat16
LEN = {"x": 4, "y": 4, "z": 8}
CHIPS = 128
OWNED = 1024
ROWS = 256
HALF = 384
CAP = 6
SHARE = 128
TILE = 256


def iota(shape, dim):
    return lax.broadcasted_iota(jnp.int32, shape, dim)


def peer(me, d):
    return lax.rem(me + d, CHIPS)


def blocks_start(src, dst, ssem, rsem, me):
    def go(d, _):
        o = peer(me, d)
        pltpu.make_async_remote_copy(
            src(o), dst(me), ssem, rsem, device_id={"dp": o}, device_id_type=MESH
        ).start()
        return 0

    lax.fori_loop(1, CHIPS, go, 0)


def wait_send(ref, ssem, rsem):
    pltpu.make_async_remote_copy(
        ref, ref, ssem, rsem, device_id={"dp": 0}, device_id_type=MESH
    ).wait_send()


def wait_recv(ref, ssem, rsem):
    pltpu.make_async_remote_copy(
        ref, ref, ssem, rsem, device_id={"dp": 0}, device_id_type=MESH
    ).wait_recv()


def make_colour(own, shards, core, ssem, rsem, at_chip, pending, count):
    def chip(axis, v):
        d = dict(at_chip)
        d[axis] = v
        return (d["y"] * 8 + d["z"]) * 4 + d["x"]

    def off(axis, k):
        return lax.rem(at_chip[axis] + k + LEN[axis], LEN[axis])

    def send(src, dst, **to):
        i = count[0]
        count[0] += 1
        copy = pltpu.make_async_remote_copy(
            src, dst, ssem.at[i], rsem.at[i], device_id=to, device_id_type=MESH
        )
        copy.start()
        pending.append(copy.wait_send)
        return i

    def arrived(ref, i):
        wait_recv(ref, ssem.at[i], rsem.at[i])

    def colour(first, second, unit):
        gathered, theirs = shards[unit].at[core], shards[unit].at[1 - core]
        c1, c2 = at_chip[first], at_chip[second]
        last = LEN[second] // 2
        n = LEN[first]

        def at(k, part=None, ref=None):
            ref = gathered if ref is None else ref
            if part is None:
                return ref.at[off(second, k)]
            return ref.at[off(second, k), pl.ds(part * (n // 2), n // 2)]

        def hand_over(k, part=None):
            block = at(k, part)
            handed.append((at(k, part, theirs), send(block, block, mp=1 - core)))

        handed = []
        mine = own[unit]
        away = [
            (d, send(mine, gathered.at[c2, c1], dp=chip(first, off(first, d))))
            for d in range(1, n)
        ]
        i = count[0]
        count[0] += 1
        local = pltpu.make_async_copy(mine, gathered.at[c2, c1], ssem.at[i])
        local.start()
        yield
        local.wait()
        for d, i in away:
            arrived(gathered.at[c2, off(first, -d)], i)
        right, left = chip(second, off(second, 1)), chip(second, off(second, -1))
        from_left, from_right = send(at(0), at(0), dp=right), send(at(0), at(0), dp=left)
        hand_over(0)
        yield
        for s in range(1, last + 1):
            part = (0, 1) if s == last else (None, None)
            on = (0, 1) if s + 1 == last else (None, None)
            arrived(at(-s, part[0]), from_left)
            if s < last:
                from_left = send(at(-s, on[0]), at(-s, on[0]), dp=right)
            arrived(at(s, part[1]), from_right)
            if s < last:
                from_right = send(at(s, on[1]), at(s, on[1]), dp=left)
            hand_over(-s, part[0])
            hand_over(s, part[1])
            yield
        for ref, i in handed:
            arrived(ref, i)

    return colour


def as_column(row, n):
    eye = iota((n, n), 0) == iota((n, n), 1)
    return jnp.sum(jnp.where(eye, row, jnp.zeros_like(row)), axis=1, keepdims=True)


def kernel(
    feat, labels, q, bank_in, old_conc, negs,
    bank_out, new_conc, loss, grad,
    bank, new_bank,
    sent, sent_ids, got, got_ids, back, returned, route, wide,
    d2_mine, d2_theirs, nb16, scaled, count_of, conc_of, mine, own0, own1,
    g0, g1, qf, acc, acc16, acc_in, stats, stats_in, pos_mine, pos_theirs,
    ag_send, ag_recv, sem,
):
    me = lax.axis_index("dp")
    core = lax.axis_index("mp")
    other = 1 - core
    at_chip = {
        "x": lax.rem(me, 4),
        "y": lax.div(me, 32),
        "z": lax.rem(lax.div(me, 4), 8),
    }

    def to_partner(src, dst, k):
        return pltpu.make_async_remote_copy(
            src, dst, sem.at[k], sem.at[k + 1], device_id={"mp": other}, device_id_type=MESH
        )

    barrier = pltpu.get_barrier_semaphore()

    def greet(d, _):
        pl.semaphore_signal(
            barrier, inc=1, device_id={"dp": peer(me, d)}, device_id_type=MESH
        )
        return 0

    lax.fori_loop(1, CHIPS, greet, 0)
    pl.semaphore_signal(barrier, inc=1, device_id={"mp": other}, device_id_type=MESH)
    beside = [
        at_chip["y"] * 32 + at_chip["z"] * 4 + lax.rem(at_chip["x"] + d, 4) for d in (1, 2, 3)
    ]
    for chip in beside:
        pl.semaphore_signal(
            barrier, inc=1, device_id={"dp": chip, "mp": other}, device_id_type=MESH
        )

    read_bank = pltpu.make_async_copy(bank_in, bank, sem.at[19])
    read_bank.start()

    def clear(k, _):
        rows = pl.ds(k * 16, 16)
        got[rows, CAP:8, 0:HALF] = jnp.zeros((16, 2, HALF), BF16)
        got[rows, :, HALF:] = jnp.ones((16, 8, 128), BF16)
        returned[rows, CAP:8, :] = jnp.zeros((16, 2, HALF), BF16)
        return 0

    lax.fori_loop(0, CHIPS // 16, clear, 0)

    lab_row = labels[...]
    own_row = lax.shift_right_logical(lab_row, 10)
    own_col = as_column(own_row.astype(F32), ROWS).astype(jnp.int32)
    same = own_col == own_row
    r_i, c_i = iota((ROWS, ROWS), 0), iota((ROWS, ROWS), 1)
    rank_row = jnp.sum(jnp.where(same & (r_i < c_i), 1.0, 0.0), axis=0, keepdims=True)
    rank_col = jnp.sum(jnp.where(same & (c_i < r_i), 1.0, 0.0), axis=1, keepdims=True)
    slot_row = own_row * 8 + rank_row.astype(jnp.int32)
    slot_col = own_col * 8 + rank_col.astype(jnp.int32)
    lab_col = as_column(lab_row.astype(F32), ROWS).astype(jnp.int32)
    id_col = jnp.bitwise_and(lab_col, OWNED - 1) + 1
    at_rank = iota((ROWS, 128), 1) == rank_col.astype(jnp.int32)
    hi = jnp.where(at_rank, lax.shift_right_logical(id_col, 5).astype(F32), 0.0).astype(BF16)
    lo = jnp.where(at_rank, jnp.bitwise_and(id_col, 31).astype(F32), 0.0).astype(BF16)
    fv = feat[...]
    for k in range(OWNED // TILE):
        r = iota((TILE, ROWS), 0) + k * TILE
        pick = jnp.where(r == slot_row, 1.0, 0.0).astype(BF16)
        rows = jnp.dot(pick, fv, preferred_element_type=F32).astype(BF16)
        sent[k * 32 : (k + 1) * 32] = rows.reshape(32, 8, HALF)
        pick = jnp.where(r == own_row * 8, 1.0, 0.0).astype(BF16)
        ids = jnp.dot(pick, hi, preferred_element_type=F32) * 32.0
        ids = ids + jnp.dot(pick, lo, preferred_element_type=F32)
        sent_ids[k * 32 : (k + 1) * 32] = ids.reshape(32, 8, 128)
    c = iota((ROWS, OWNED), 1)
    route[...] = jnp.where(c == slot_col, 1.0, 0.0).astype(BF16)

    pl.semaphore_wait(barrier, CHIPS + 3)

    six = pl.ds(0, CAP)
    left = pl.ds(0, HALF)
    blocks_start(
        lambda o: sent_ids.at[o, pl.ds(0, 1)], lambda o: got_ids.at[o, pl.ds(0, 1)],
        sem.at[0], sem.at[1], me,
    )
    blocks_start(
        lambda o: sent.at[o, six], lambda o: got.at[o, six, left],
        sem.at[2], sem.at[3], me,
    )
    x = at_chip["x"]
    for chip in beside:
        for c in range(2):
            pltpu.make_async_remote_copy(
                q.at[c], qf.at[core * 4 + x], sem.at[8], sem.at[9],
                device_id={"dp": chip, "mp": c}, device_id_type=MESH,
            ).start()
    to_partner(q.at[other], qf.at[core * 4 + x], 8).start()
    home = [
        pltpu.make_async_copy(sent_ids.at[me, pl.ds(0, 1)], got_ids.at[me, pl.ds(0, 1)], sem.at[10]),
        pltpu.make_async_copy(sent.at[me, six], got.at[me, six, left], sem.at[11]),
        pltpu.make_async_copy(q.at[core], qf.at[core * 4 + x], sem.at[12]),
    ]
    for copy in home:
        copy.start()
    for copy in home:
        copy.wait()
    rest = pl.ds(0, CHIPS - 1)
    wait_recv(got_ids.at[rest, pl.ds(0, 1)], sem.at[0], sem.at[1])

    spread = jnp.broadcast_to(got_ids[:, 0:1, :], (CHIPS, 8, 128))
    here = iota((CHIPS, 8, 128), 1) == iota((CHIPS, 8, 128), 2)
    id_c = jnp.sum(jnp.where(here, spread, 0.0), axis=2, keepdims=True) - 1.0
    wide[...] = jnp.broadcast_to(id_c, (CHIPS, 8, 128)).reshape(OWNED, 128)
    id_row = jnp.transpose(wide[...])[0:1, :].astype(jnp.int32)
    wait_recv(got.at[rest, six, left], sem.at[2], sem.at[3])

    read_bank.wait()
    gv = got[...].reshape(OWNED, HALF + 128)
    for k in range(OWNED // TILE):
        rows = pl.ds(k * TILE, TILE)
        hit = jnp.where(iota((TILE, OWNED), 0) + k * TILE == id_row, 1.0, 0.0).astype(BF16)
        sums = jnp.dot(hit, gv, preferred_element_type=F32)
        counts = sums[:, HALF : HALF + 1]
        old = bank[rows, :]
        mixed = 0.5 * old + 0.5 * sums[:, 0:HALF] / jnp.maximum(counts, 1.0)
        fresh = jnp.where(counts > 0, mixed, old)
        new_bank[rows, :] = fresh
        nb16[rows, :] = fresh.astype(BF16)
        count_of[rows, :] = sums[:, HALF:]

    nbv = nb16[...]
    for k in range(OWNED // TILE):
        rows = pl.ds(k * TILE, TILE)
        ids = wide[rows, :][:, 0:1].astype(jnp.int32)
        hit = jnp.where(iota((TILE, OWNED), 1) == ids, 1.0, 0.0).astype(BF16)
        near = jnp.dot(hit, nbv, preferred_element_type=F32)
        apart = got[k * 32 : (k + 1) * 32, :, 0:HALF].reshape(TILE, HALF).astype(F32) - near
        d2 = jnp.sum(apart * apart, axis=1, keepdims=True)
        d2_mine[:, k * TILE : (k + 1) * TILE] = jnp.transpose(jnp.broadcast_to(d2, (TILE, 128)))[0:8, :]
    write_bank = pltpu.make_async_copy(new_bank, bank_out, sem.at[20])
    write_bank.start()
    d2x = to_partner(d2_mine, d2_theirs, 13)
    d2x.start()
    neg_row = negs[pl.ds(lax.div(me, 2), 1), :]
    want = as_column(neg_row.astype(F32), 128).astype(jnp.int32) - me * OWNED
    old_col = jnp.transpose(jnp.broadcast_to(old_conc[...], (128, OWNED)))
    conc_of[...] = old_col
    d2x.wait()

    dist = jnp.sqrt(d2_mine[0:1, :] + d2_theirs[0:1, :] + 0.25)
    for k in range(OWNED // TILE):
        rows = pl.ds(k * TILE, TILE)
        on = iota((TILE, OWNED), 0) + k * TILE == id_row
        total = jnp.sum(jnp.where(on, dist, 0.0), axis=1, keepdims=True)
        counts = count_of[rows, :][:, 0:1]
        safe = jnp.maximum(counts, 1.0)
        conc = jnp.where(counts > 0, total / (safe * jnp.log(safe + 10.0)), conc_of[rows, :][:, 0:1])
        scaled[rows, :] = (new_bank[rows, :] / conc).astype(BF16)
        conc_of[rows, :] = jnp.broadcast_to(conc, (TILE, 128))

    sv = scaled[...]
    hit = jnp.where(iota((128, OWNED), 1) == want, 1.0, 0.0).astype(BF16)
    mine[...] = jnp.dot(hit, sv, preferred_element_type=F32).astype(BF16).reshape(8, 16, HALF)
    base = lax.rem(me, 2) * 4
    swap = []
    for k, own in enumerate((own0, own1)):
        swap.append(to_partner(mine.at[base + other * 2 + k], own.at[core], 21 + 2 * k))
        swap[-1].start()
    keep = [
        pltpu.make_async_copy(mine.at[base + core * 2 + k], own.at[core], sem.at[15 + k])
        for k, own in enumerate((own0, own1))
    ]
    for copy in keep:
        copy.start()
    for copy in keep:
        copy.wait()
    new_conc[...] = jnp.transpose(conc_of[...])[0:1, :]
    for copy in swap:
        copy.wait()

    pending = []
    count = [0]
    colour = make_colour((own0, own1), (g0, g1), core, ag_send, ag_recv, at_chip, pending, count)
    live = [colour("z", "y", 0), colour("y", "z", 1)]

    def advance():
        for g in list(live):
            try:
                next(g)
            except StopIteration:
                live.remove(g)

    advance()

    for k in range(OWNED // TILE):
        rows = pl.ds(k * TILE, TILE)
        ids = wide[rows, :][:, 0:1].astype(jnp.int32)
        hit = jnp.where(iota((TILE, OWNED), 1) == ids, 1.0, 0.0).astype(BF16)
        out = jnp.dot(hit, sv, preferred_element_type=F32).astype(BF16)
        back[k * 32 : (k + 1) * 32] = out.reshape(32, 8, HALF)
    advance()
    blocks_start(
        lambda o: back.at[o, six], lambda o: returned.at[o, six],
        sem.at[4], sem.at[5], me,
    )
    copy = pltpu.make_async_copy(back.at[me, six], returned.at[me, six], sem.at[18])
    copy.start()
    copy.wait()
    while live:
        advance()

    seven = qf.at[pl.ds(0, 7)]
    wait_recv(seven, sem.at[8], sem.at[9])
    wait_send(seven, sem.at[8], sem.at[9])
    many = 4 * SHARE
    q0, q1 = qf[0:4].reshape(many, HALF), qf[4:8].reshape(many, HALF)
    top = jnp.full((many, 1), -3.0e38, F32)
    sums = jnp.zeros((many, 1), F32)
    acc[...] = jnp.zeros((2, many, HALF), F32)
    nt = (((1,), (1,)), ((), ()))
    for g, planes, width in ((g0, 4, 1), (g1, 4, 2)):
        for k in range(planes):
            part = pl.ds(k * width, width)
            k0 = g[:, part, :, 0].reshape(TILE, HALF)
            k1 = g[:, part, :, 1].reshape(TILE, HALF)
            s = lax.dot_general(q0, k0, nt, preferred_element_type=F32)
            s = s + lax.dot_general(q1, k1, nt, preferred_element_type=F32)
            higher = jnp.maximum(top, jnp.max(s, axis=1, keepdims=True))
            shrink = jnp.exp(top - higher)
            p = jnp.exp(s - higher)
            sums = sums * shrink + jnp.sum(p, axis=1, keepdims=True)
            pb = p.astype(BF16)
            acc[0] = acc[0] * shrink + jnp.dot(pb, k0, preferred_element_type=F32)
            acc[1] = acc[1] * shrink + jnp.dot(pb, k1, preferred_element_type=F32)
            top = higher
    acc16[...] = acc[...].astype(BF16).reshape(2, 4, SHARE, HALF)
    lane = iota((many, 128), 1)
    both = jnp.transpose(jnp.where(lane == 0, top, sums))
    for k in range(4):
        stats[k] = both[0:8, k * SHARE : (k + 1) * SHARE]

    for chip, d in zip(beside, (1, 2, 3)):
        there = lax.rem(x + d, 4)
        for h in range(2):
            to = {"dp": chip, "mp": h}
            pltpu.make_async_remote_copy(
                stats.at[there], stats_in.at[x * 2 + core], sem.at[27], sem.at[28], device_id=to, device_id_type=MESH
            ).start()
            pltpu.make_async_remote_copy(
                acc16.at[h, there], acc_in.at[x * 2 + core], sem.at[25], sem.at[26], device_id=to, device_id_type=MESH
            ).start()
    to_partner(stats.at[x], stats_in.at[x * 2 + core], 27).start()
    to_partner(acc16.at[other, x], acc_in.at[x * 2 + core], 25).start()
    keep = [
        pltpu.make_async_copy(stats.at[x], stats_in.at[x * 2 + core], sem.at[29]),
        pltpu.make_async_copy(acc16.at[core, x], acc_in.at[x * 2 + core], sem.at[30]),
    ]
    for copy in keep:
        copy.start()

    wait_recv(returned.at[rest, six], sem.at[4], sem.at[5])
    pos_rows = jnp.dot(
        route[...], returned[...].reshape(OWNED, HALF), preferred_element_type=F32
    )
    part = jnp.sum(q[...].reshape(ROWS, HALF).astype(F32) * pos_rows, axis=1, keepdims=True)
    pos_mine[...] = jnp.transpose(jnp.broadcast_to(part, (ROWS, 128)))[0:8, :]
    px = to_partner(pos_mine, pos_theirs, 31)
    px.start()
    px.wait()
    positive_row = pos_mine[0:1, :] + pos_theirs[0:1, :]
    for copy in keep:
        copy.wait()
    for ref, k in ((stats_in, 27), (acc_in, 25)):
        wait_recv(ref.at[pl.ds(0, 7)], sem.at[k], sem.at[k + 1])
        wait_send(ref.at[pl.ds(0, 7)], sem.at[k], sem.at[k + 1])
    for c in range(2):
        rows = slice(c * SHARE, (c + 1) * SHARE)
        positive = positive_row[:, rows]
        tops = [stats_in[k * 2 + c, 0:1, :] for k in range(4)]
        peak = positive
        for t in tops:
            peak = jnp.maximum(peak, t)
        weights = [jnp.exp(t - peak) for t in tops]
        wp = jnp.exp(positive - peak)
        total = wp
        for k in range(4):
            total = total + stats_in[k * 2 + c, 1:2, :] * weights[k]
        loss[:, rows] = jnp.log(total) + peak - positive
        out = as_column(wp / total - 1.0, SHARE) * pos_rows[rows]
        for k in range(4):
            out = out + as_column(weights[k] / total, SHARE) * acc_in[k * 2 + c].astype(F32)
        grad[rows, :] = out

    write_bank.wait()
    for wait in pending:
        wait()
    wait_send(sent_ids.at[rest, pl.ds(0, 1)], sem.at[0], sem.at[1])
    wait_send(sent.at[rest, six], sem.at[2], sem.at[3])
    wait_send(back.at[rest, six], sem.at[4], sem.at[5])


def body(features, labels, queries, bank, old_conc, neg_index):
    vmem = pl.BlockSpec(memory_space=pltpu.VMEM)
    hbm = pl.BlockSpec(memory_space=pl.ANY)
    outs = pl.pallas_call(
        kernel,
        out_shape=(
            jax.ShapeDtypeStruct((OWNED, HALF), F32),
            jax.ShapeDtypeStruct((1, OWNED), F32),
            jax.ShapeDtypeStruct((1, ROWS), F32),
            jax.ShapeDtypeStruct((ROWS, HALF), F32),
        ),
        in_specs=[vmem, vmem, vmem, hbm, vmem, vmem],
        out_specs=(hbm, vmem, vmem, vmem),
        scratch_shapes=[
            pltpu.VMEM((OWNED, HALF), F32),
            pltpu.VMEM((OWNED, HALF), F32),
            pltpu.VMEM((CHIPS, 8, HALF), BF16),
            pltpu.VMEM((CHIPS, 8, 128), F32),
            pltpu.VMEM((CHIPS, 8, HALF + 128), BF16),
            pltpu.VMEM((CHIPS, 8, 128), F32),
            pltpu.VMEM((CHIPS, 8, HALF), BF16),
            pltpu.VMEM((CHIPS, 8, HALF), BF16),
            pltpu.VMEM((ROWS, OWNED), BF16),
            pltpu.VMEM((OWNED, 128), F32),
            pltpu.VMEM((8, OWNED), F32),
            pltpu.VMEM((8, OWNED), F32),
            pltpu.VMEM((OWNED, HALF), BF16),
            pltpu.VMEM((OWNED, HALF), BF16),
            pltpu.VMEM((OWNED, 128), F32),
            pltpu.VMEM((OWNED, 128), F32),
            pltpu.VMEM((8, 16, HALF), BF16),
            pltpu.VMEM((2, 16, HALF), BF16),
            pltpu.VMEM((2, 16, HALF), BF16),
            pltpu.VMEM((2, 4, 8, 2, 16, HALF), BF16),
            pltpu.VMEM((2, 8, 4, 2, 16, HALF), BF16),
            pltpu.VMEM((8, SHARE, HALF), BF16),
            pltpu.VMEM((2, 4 * SHARE, HALF), F32),
            pltpu.VMEM((2, 4, SHARE, HALF), BF16),
            pltpu.VMEM((8, SHARE, HALF), BF16),
            pltpu.VMEM((4, 8, SHARE), F32),
            pltpu.VMEM((8, 8, SHARE), F32),
            pltpu.VMEM((8, ROWS), F32),
            pltpu.VMEM((8, ROWS), F32),
            pltpu.SemaphoreType.DMA((64,)),
            pltpu.SemaphoreType.DMA((64,)),
            pltpu.SemaphoreType.DMA((40,)),
        ],
        compiler_params=pltpu.CompilerParams(
            collective_id=0, has_side_effects=True, vmem_limit_bytes=32 << 20
        ),
        name="step",
    )(
        features,
        labels.reshape(1, ROWS),
        queries.reshape(2, SHARE, HALF),
        bank,
        old_conc.reshape(1, OWNED),
        neg_index.reshape(64, 128),
    )
    new_bank, new_conc, loss, grad = outs
    return new_bank, new_conc.reshape(OWNED), loss.reshape(ROWS), grad


def solution(mesh):
    return jax.shard_map(
        body,
        mesh=mesh,
        in_specs=(P("dp", "mp"), P("dp"), P("dp", "mp"), P("dp", "mp"), P("dp"), P()),
        out_specs=(P("dp", "mp"), P("dp"), P("dp"), P("dp", "mp")),
        check_vma=False,
    )
```

time: 103 us -> 99.9 us (0.970)
  Pallas kernels: 97.5 us -> 90.5 us
  local copies, waits for them, and re-layouts: 4.62 us -> 8.42 us
    pallas_call x1, Pallas kernels: 97.5 us -> 90.5 us  [body(): pl.pallas_call(kernel, out_shape=(jax.ShapeDtypeStruct((OWNED, HALF), F32...]
    unnamed x10 -> x16, local copies, waits for them, and re-layouts: 4.62 us -> 8.42 us
where the time goes in v2:
time: 99.9 us; the launch traced here: 99.6 us
  Pallas kernels  90.5 us (91%)
  local copies, waits for them, and re-layouts  8.42 us (8%)
    pallas_call x1, Pallas kernels, body(): pl.pallas_call(kernel, out_shape=(jax.ShapeDtypeStruct((OWNED, HALF), F32...  90.5 us
    unnamed x16, local copies, waits for them, and re-layouts  8.42 us

profile of v2, /device:TPU:1, one launch (start us, length us, event | category | flops | bytes accessed | tf_op | source)
XLA Modules:
  0.0 99.6 jit_solution(15661537580037624077)
XLA Ops:
  0.6 0.0 copy-start
  0.6 1.4 %copy-done = f32[1024,384]{1,0:T(8,128)S(1)} copy-done((f32[1024,384]{1,0:T(8,128)S(1)}, f32[1024,384]{1,0:T(8,128)}, u32[]{:S(2)}) %copy-start) | copy-done | bytes 1572888
  2.0 0.0 copy-start.1
  2.0 0.9 copy-done.1
  3.0 0.0 copy-start.2
  3.0 0.9 copy-done.2
  3.9 0.0 copy-start.3
  3.9 0.8 copy-done.3
  4.7 0.0 copy-start.4
  4.7 0.7 copy-done.4
  5.3 0.0 copy-start.5
  5.3 0.7 copy-done.5
  6.0 90.5 %step.1 = (f32[1024,384]{1,0:T(8,128)S(1)}, f32[1,1024]{1,0:T(1,128)S(1)}, f32[1,256]{1,0:T(1,128)S(1)}, f32[256,384]{1,0:T(8,128)S(1)}) custom-call(bf16[256,384]{1,0:T(8,128)(2,1)S(1)} %copy-done.1, s32[1,256]{1,0:T(1,128)S(1)} %bitcast.10, bf16[2,128,384]{2,1,0:T(8,128)(2,1)S(1)} %bitcast.6, f32[1024,384]{1,0:T(8,128)S(1)} %copy-done, ...), custom_call_target="tpu_custom_call" | custom-call | tf_op jit(solution)/shard_map/step/pallas_call | solution.py:438
  96.5 1.1 %copy.14 = f32[1024,384]{1,0:T(8,128)} copy(f32[1024,384]{1,0:T(8,128)S(1)} %get-tuple-element.16) | data formatting | bytes 3145728
  97.7 0.6 copy.15
  98.3 0.6 copy.16
  98.8 0.7 copy.17
Async XLA Ops:
  0.6 1.4 %copy-start = (f32[1024,384]{1,0:T(8,128)S(1)}, f32[1024,384]{1,0:T(8,128)}, u32[]{:S(2)}) copy-start(f32[1024,384]{1,0:T(8,128)} %bank_in.1) | copy-start | bytes 4718596
  2.0 0.9 copy-start.1
  3.0 0.9 copy-start.2
  3.9 0.8 copy-start.3
  4.7 0.7 copy-start.4
  5.3 0.7 copy-start.5

commit v3 on v2

--- a/solution.py
+++ b/solution.py
@@ -49,14 +49,17 @@
     ).wait_recv()
 
 
-def make_colour(own, shards, core, ssem, rsem, at_chip, pending, count):
-    def chip(axis, v):
+def gather_rounds(mine, gathered, theirs, core, ssem, rsem, at_chip, pending):
+    count = [0]
+    lengths = {"y": LEN["y"], "z": LEN["z"]}
+
+    def off(axis, k):
+        return lax.rem(at_chip[axis] + k + lengths[axis], lengths[axis])
+
+    def chip(axis, k):
         d = dict(at_chip)
-        d[axis] = v
+        d[axis] = off(axis, k)
         return (d["y"] * 8 + d["z"]) * 4 + d["x"]
-
-    def off(axis, k):
-        return lax.rem(at_chip[axis] + k + LEN[axis], LEN[axis])
 
     def send(src, dst, **to):
         i = count[0]
@@ -71,56 +74,71 @@
     def arrived(ref, i):
         wait_recv(ref, ssem.at[i], rsem.at[i])
 
-    def colour(first, second, unit):
-        gathered, theirs = shards[unit].at[core], shards[unit].at[1 - core]
-        c1, c2 = at_chip[first], at_chip[second]
-        last = LEN[second] // 2
-        n = LEN[first]
-
-        def at(k, part=None, ref=None):
-            ref = gathered if ref is None else ref
-            if part is None:
-                return ref.at[off(second, k)]
-            return ref.at[off(second, k), pl.ds(part * (n // 2), n // 2)]
-
-        def hand_over(k, part=None):
-            block = at(k, part)
-            handed.append((at(k, part, theirs), send(block, block, mp=1 - core)))
-
-        handed = []
-        mine = own[unit]
-        away = [
-            (d, send(mine, gathered.at[c2, c1], dp=chip(first, off(first, d))))
-            for d in range(1, n)
-        ]
-        i = count[0]
-        count[0] += 1
-        local = pltpu.make_async_copy(mine, gathered.at[c2, c1], ssem.at[i])
-        local.start()
+    def at(y, z, half=None, ref=gathered):
+        ref = ref.at[off("y", y), off("z", z)]
+        return ref if half is None else ref.at[half]
+
+    handed = []
+
+    def hand_over(y, z):
+        handed.append((at(y, z, ref=theirs), send(at(y, z), at(y, z), mp=1 - core)))
+
+    flying = {}
+
+    def along_y(z, src=None):
+        src = at(0, z) if src is None else src
+        flying[z] = (send(src, at(0, z), dp=chip("y", 1)), send(src, at(0, z), dp=chip("y", -1)))
+
+    def on_y(z):
+        arrived(at(-1, z), flying[z][0])
+        right = send(at(-1, z, 0), at(-1, z, 0), dp=chip("y", 1))
+        arrived(at(1, z), flying[z][1])
+        flying[z] = (right, send(at(1, z, 1), at(1, z, 1), dp=chip("y", -1)))
+        hand_over(-1, z)
+        hand_over(1, z)
+
+    def end_y(z):
+        arrived(at(2, z, 0), flying[z][0])
+        arrived(at(2, z, 1), flying[z][1])
+        hand_over(2, z)
+
+    up, down = chip("z", 1), chip("z", -1)
+    from_down, from_up = send(mine, at(0, 0), dp=up), send(mine, at(0, 0), dp=down)
+    along_y(0, mine)
+    i = count[0]
+    count[0] += 1
+    local = pltpu.make_async_copy(mine, at(0, 0), ssem.at[i])
+    local.start()
+    local.wait()
+    hand_over(0, 0)
+    yield
+    for s in (1, 2, 3):
+        part = (0, 1) if s == 3 else (None, None)
+        arrived(at(0, -s), from_down)
+        from_down = send(at(0, -s, part[0]), at(0, -s, part[0]), dp=up)
+        arrived(at(0, s), from_up)
+        from_up = send(at(0, s, part[1]), at(0, s, part[1]), dp=down)
+        along_y(-s)
+        along_y(s)
+        hand_over(0, -s)
+        hand_over(0, s)
+        for z in ((0,), (-1, 1), (-2, 2))[s - 1]:
+            on_y(z)
         yield
-        local.wait()
-        for d, i in away:
-            arrived(gathered.at[c2, off(first, -d)], i)
-        right, left = chip(second, off(second, 1)), chip(second, off(second, -1))
-        from_left, from_right = send(at(0), at(0), dp=right), send(at(0), at(0), dp=left)
-        hand_over(0)
-        yield
-        for s in range(1, last + 1):
-            part = (0, 1) if s == last else (None, None)
-            on = (0, 1) if s + 1 == last else (None, None)
-            arrived(at(-s, part[0]), from_left)
-            if s < last:
-                from_left = send(at(-s, on[0]), at(-s, on[0]), dp=right)
-            arrived(at(s, part[1]), from_right)
-            if s < last:
-                from_right = send(at(s, on[1]), at(s, on[1]), dp=left)
-            hand_over(-s, part[0])
-            hand_over(s, part[1])
-            yield
-        for ref, i in handed:
-            arrived(ref, i)
-
-    return colour
+    arrived(at(0, 4, 0), from_down)
+    arrived(at(0, 4, 1), from_up)
+    along_y(4)
+    hand_over(0, 4)
+    for z in (-3, 3):
+        on_y(z)
+    for z in (0, -1, 1):
+        end_y(z)
+    on_y(4)
+    yield
+    for z in (-2, 2, -3, 3, 4):
+        end_y(z)
+    for ref, i in handed:
+        arrived(ref, i)
 
 
 def as_column(row, n):
@@ -129,12 +147,12 @@
 
 
 def kernel(
-    feat, labels, q, bank_in, old_conc, negs,
-    bank_out, new_conc, loss, grad,
-    bank, new_bank,
+    feat_in, labels_in, q_in, bank_in, old_conc_in, negs_in,
+    new_bank, new_conc, loss, grad,
+    feat, labels, q, bank, old_conc, negs,
     sent, sent_ids, got, got_ids, back, returned, route, wide,
-    d2_mine, d2_theirs, nb16, scaled, count_of, conc_of, mine, own0, own1,
-    g0, g1, qf, acc, acc16, acc_in, stats, stats_in, pos_mine, pos_theirs,
+    d2_mine, d2_theirs, nb16, scaled, count_of, conc_of, mine, own,
+    shards, qf, acc, acc16, acc_in, stats, stats_in, pos_mine, pos_theirs,
     ag_send, ag_recv, sem,
 ):
     me = lax.axis_index("dp")
@@ -151,15 +169,31 @@
             src, dst, sem.at[k], sem.at[k + 1], device_id={"mp": other}, device_id_type=MESH
         )
 
+    reads = [
+        pltpu.make_async_copy(src, dst, sem.at[k])
+        for src, dst, k in (
+            (labels_in, labels, 33), (feat_in, feat, 34), (q_in, q, 35),
+            (old_conc_in, old_conc, 36), (negs_in, negs, 37), (bank_in, bank, 38),
+        )
+    ]
+    for copy in reads:
+        copy.start()
+
     barrier = pltpu.get_barrier_semaphore()
 
-    def greet(d, _):
-        pl.semaphore_signal(
-            barrier, inc=1, device_id={"dp": peer(me, d)}, device_id_type=MESH
-        )
-        return 0
-
-    lax.fori_loop(1, CHIPS, greet, 0)
+    hops = sorted(
+        ((min(dx, 4 - dx) + min(dy, 4 - dy) + min(dz, 8 - dz), dx, dy, dz)
+         for dx in range(4) for dy in range(4) for dz in range(8)),
+        reverse=True,
+    )
+    xs = [lax.rem(at_chip["x"] + d, 4) for d in range(4)]
+    ys = [lax.rem(at_chip["y"] + d, 4) * 32 for d in range(4)]
+    zs = [lax.rem(at_chip["z"] + d, 8) * 4 for d in range(8)]
+    for far, dx, dy, dz in hops:
+        if far:
+            pl.semaphore_signal(
+                barrier, inc=1, device_id={"dp": ys[dy] + zs[dz] + xs[dx]}, device_id_type=MESH
+            )
     pl.semaphore_signal(barrier, inc=1, device_id={"mp": other}, device_id_type=MESH)
     beside = [
         at_chip["y"] * 32 + at_chip["z"] * 4 + lax.rem(at_chip["x"] + d, 4) for d in (1, 2, 3)
@@ -169,9 +203,6 @@
             barrier, inc=1, device_id={"dp": chip, "mp": other}, device_id_type=MESH
         )
 
-    read_bank = pltpu.make_async_copy(bank_in, bank, sem.at[19])
-    read_bank.start()
-
     def clear(k, _):
         rows = pl.ds(k * 16, 16)
         got[rows, CAP:8, 0:HALF] = jnp.zeros((16, 2, HALF), BF16)
@@ -180,6 +211,9 @@
         return 0
 
     lax.fori_loop(0, CHIPS // 16, clear, 0)
+
+    for copy in reads[:3]:
+        copy.wait()
 
     lab_row = labels[...]
     own_row = lax.shift_right_logical(lab_row, 10)
@@ -247,7 +281,8 @@
     id_row = jnp.transpose(wide[...])[0:1, :].astype(jnp.int32)
     wait_recv(got.at[rest, six, left], sem.at[2], sem.at[3])
 
-    read_bank.wait()
+    for copy in reads[3:]:
+        copy.wait()
     gv = got[...].reshape(OWNED, HALF + 128)
     for k in range(OWNED // TILE):
         rows = pl.ds(k * TILE, TILE)
@@ -270,8 +305,6 @@
         apart = got[k * 32 : (k + 1) * 32, :, 0:HALF].reshape(TILE, HALF).astype(F32) - near
         d2 = jnp.sum(apart * apart, axis=1, keepdims=True)
         d2_mine[:, k * TILE : (k + 1) * TILE] = jnp.transpose(jnp.broadcast_to(d2, (TILE, 128)))[0:8, :]
-    write_bank = pltpu.make_async_copy(new_bank, bank_out, sem.at[20])
-    write_bank.start()
     d2x = to_partner(d2_mine, d2_theirs, 13)
     d2x.start()
     neg_row = negs[pl.ds(lax.div(me, 2), 1), :]
@@ -293,37 +326,21 @@
 
     sv = scaled[...]
     hit = jnp.where(iota((128, OWNED), 1) == want, 1.0, 0.0).astype(BF16)
-    mine[...] = jnp.dot(hit, sv, preferred_element_type=F32).astype(BF16).reshape(8, 16, HALF)
-    base = lax.rem(me, 2) * 4
-    swap = []
-    for k, own in enumerate((own0, own1)):
-        swap.append(to_partner(mine.at[base + other * 2 + k], own.at[core], 21 + 2 * k))
-        swap[-1].start()
-    keep = [
-        pltpu.make_async_copy(mine.at[base + core * 2 + k], own.at[core], sem.at[15 + k])
-        for k, own in enumerate((own0, own1))
-    ]
-    for copy in keep:
-        copy.start()
-    for copy in keep:
-        copy.wait()
+    mine[...] = jnp.dot(hit, sv, preferred_element_type=F32).astype(BF16).reshape(4, 32, HALF)
+    base = lax.rem(me, 2) * 2
+    swap = to_partner(mine.at[base + other], own.at[core], 21)
+    swap.start()
+    keep = pltpu.make_async_copy(mine.at[base + core], own.at[core], sem.at[15])
+    keep.start()
+    keep.wait()
     new_conc[...] = jnp.transpose(conc_of[...])[0:1, :]
-    for copy in swap:
-        copy.wait()
+    swap.wait()
 
     pending = []
-    count = [0]
-    colour = make_colour((own0, own1), (g0, g1), core, ag_send, ag_recv, at_chip, pending, count)
-    live = [colour("z", "y", 0), colour("y", "z", 1)]
-
-    def advance():
-        for g in list(live):
-            try:
-                next(g)
-            except StopIteration:
-                live.remove(g)
-
-    advance()
+    rounds = gather_rounds(
+        own, shards.at[core], shards.at[other], core, ag_send, ag_recv, at_chip, pending
+    )
+    next(rounds)
 
     for k in range(OWNED // TILE):
         rows = pl.ds(k * TILE, TILE)
@@ -331,7 +348,7 @@
         hit = jnp.where(iota((TILE, OWNED), 1) == ids, 1.0, 0.0).astype(BF16)
         out = jnp.dot(hit, sv, preferred_element_type=F32).astype(BF16)
         back[k * 32 : (k + 1) * 32] = out.reshape(32, 8, HALF)
-    advance()
+    next(rounds)
     blocks_start(
         lambda o: back.at[o, six], lambda o: returned.at[o, six],
         sem.at[4], sem.at[5], me,
@@ -339,23 +356,24 @@
     copy = pltpu.make_async_copy(back.at[me, six], returned.at[me, six], sem.at[18])
     copy.start()
     copy.wait()
-    while live:
-        advance()
+    for _ in rounds:
+        pass
 
     seven = qf.at[pl.ds(0, 7)]
     wait_recv(seven, sem.at[8], sem.at[9])
     wait_send(seven, sem.at[8], sem.at[9])
-    many = 4 * SHARE
-    q0, q1 = qf[0:4].reshape(many, HALF), qf[4:8].reshape(many, HALF)
-    top = jnp.full((many, 1), -3.0e38, F32)
-    sums = jnp.zeros((many, 1), F32)
-    acc[...] = jnp.zeros((2, many, HALF), F32)
+    many = 2 * SHARE
     nt = (((1,), (1,)), ((), ()))
-    for g, planes, width in ((g0, 4, 1), (g1, 4, 2)):
-        for k in range(planes):
-            part = pl.ds(k * width, width)
-            k0 = g[:, part, :, 0].reshape(TILE, HALF)
-            k1 = g[:, part, :, 1].reshape(TILE, HALF)
+    lane = iota((many, 128), 1)
+    for far in ((2, 1), (3, 0)):
+        chips = [lax.rem(x + d, 4) for d in far]
+        q0 = jnp.concatenate([qf[c] for c in chips], axis=0)
+        q1 = jnp.concatenate([qf[4 + c] for c in chips], axis=0)
+        top = jnp.full((many, 1), -3.0e38, F32)
+        sums = jnp.zeros((many, 1), F32)
+        for y in range(4):
+            k0 = shards[:, y, :, 0].reshape(2 * TILE, HALF)
+            k1 = shards[:, y, :, 1].reshape(2 * TILE, HALF)
             s = lax.dot_general(q0, k0, nt, preferred_element_type=F32)
             s = s + lax.dot_general(q1, k1, nt, preferred_element_type=F32)
             higher = jnp.maximum(top, jnp.max(s, axis=1, keepdims=True))
@@ -363,25 +381,28 @@
             p = jnp.exp(s - higher)
             sums = sums * shrink + jnp.sum(p, axis=1, keepdims=True)
             pb = p.astype(BF16)
-            acc[0] = acc[0] * shrink + jnp.dot(pb, k0, preferred_element_type=F32)
-            acc[1] = acc[1] * shrink + jnp.dot(pb, k1, preferred_element_type=F32)
+            for h, kh in ((0, k0), (1, k1)):
+                more = jnp.dot(pb, kh, preferred_element_type=F32)
+                acc[h] = more if y == 0 else acc[h] * shrink + more
             top = higher
-    acc16[...] = acc[...].astype(BF16).reshape(2, 4, SHARE, HALF)
-    lane = iota((many, 128), 1)
-    both = jnp.transpose(jnp.where(lane == 0, top, sums))
-    for k in range(4):
-        stats[k] = both[0:8, k * SHARE : (k + 1) * SHARE]
-
-    for chip, d in zip(beside, (1, 2, 3)):
-        there = lax.rem(x + d, 4)
-        for h in range(2):
-            to = {"dp": chip, "mp": h}
-            pltpu.make_async_remote_copy(
-                stats.at[there], stats_in.at[x * 2 + core], sem.at[27], sem.at[28], device_id=to, device_id_type=MESH
-            ).start()
-            pltpu.make_async_remote_copy(
-                acc16.at[h, there], acc_in.at[x * 2 + core], sem.at[25], sem.at[26], device_id=to, device_id_type=MESH
-            ).start()
+        both = jnp.transpose(jnp.where(lane == 0, top, sums))
+        for k, c in enumerate(chips):
+            stats[c] = both[0:8, k * SHARE : (k + 1) * SHARE]
+            for h in range(2):
+                acc16[h, c] = acc[h, k * SHARE : (k + 1) * SHARE].astype(BF16)
+        for d, c in zip(far, chips):
+            if d == 0:
+                continue
+            for h in range(2):
+                to = {"dp": beside[d - 1], "mp": h}
+                pltpu.make_async_remote_copy(
+                    acc16.at[h, c], acc_in.at[x * 2 + core], sem.at[25], sem.at[26],
+                    device_id=to, device_id_type=MESH,
+                ).start()
+                pltpu.make_async_remote_copy(
+                    stats.at[c], stats_in.at[x * 2 + core], sem.at[27], sem.at[28],
+                    device_id=to, device_id_type=MESH,
+                ).start()
     to_partner(stats.at[x], stats_in.at[x * 2 + core], 27).start()
     to_partner(acc16.at[other, x], acc_in.at[x * 2 + core], 25).start()
     keep = [
@@ -424,7 +445,6 @@
             out = out + as_column(weights[k] / total, SHARE) * acc_in[k * 2 + c].astype(F32)
         grad[rows, :] = out
 
-    write_bank.wait()
     for wait in pending:
         wait()
     wait_send(sent_ids.at[rest, pl.ds(0, 1)], sem.at[0], sem.at[1])
@@ -432,9 +452,17 @@
     wait_send(back.at[rest, six], sem.at[4], sem.at[5])
 
 
+def hand_out(*refs):
+    copies = [pltpu.make_async_copy(refs[k], refs[4 + k], refs[8].at[k]) for k in range(4)]
+    for copy in copies:
+        copy.start()
+    for copy in copies:
+        copy.wait()
+
+
 def body(features, labels, queries, bank, old_conc, neg_index):
     vmem = pl.BlockSpec(memory_space=pltpu.VMEM)
-    hbm = pl.BlockSpec(memory_space=pl.ANY)
+    hbm = pl.BlockSpec(memory_space=pltpu.HBM)
     outs = pl.pallas_call(
         kernel,
         out_shape=(
@@ -443,11 +471,15 @@
             jax.ShapeDtypeStruct((1, ROWS), F32),
             jax.ShapeDtypeStruct((ROWS, HALF), F32),
         ),
-        in_specs=[vmem, vmem, vmem, hbm, vmem, vmem],
-        out_specs=(hbm, vmem, vmem, vmem),
+        in_specs=[hbm] * 6,
+        out_specs=(vmem,) * 4,
         scratch_shapes=[
+            pltpu.VMEM((ROWS, HALF), BF16),
+            pltpu.VMEM((1, ROWS), jnp.int32),
+            pltpu.VMEM((2, SHARE, HALF), BF16),
             pltpu.VMEM((OWNED, HALF), F32),
-            pltpu.VMEM((OWNED, HALF), F32),
+            pltpu.VMEM((1, OWNED), F32),
+            pltpu.VMEM((64, 128), jnp.int32),
             pltpu.VMEM((CHIPS, 8, HALF), BF16),
             pltpu.VMEM((CHIPS, 8, 128), F32),
             pltpu.VMEM((CHIPS, 8, HALF + 128), BF16),
@@ -462,21 +494,19 @@
             pltpu.VMEM((OWNED, HALF), BF16),
             pltpu.VMEM((OWNED, 128), F32),
             pltpu.VMEM((OWNED, 128), F32),
-            pltpu.VMEM((8, 16, HALF), BF16),
-            pltpu.VMEM((2, 16, HALF), BF16),
-            pltpu.VMEM((2, 16, HALF), BF16),
-            pltpu.VMEM((2, 4, 8, 2, 16, HALF), BF16),
-            pltpu.VMEM((2, 8, 4, 2, 16, HALF), BF16),
+            pltpu.VMEM((4, 32, HALF), BF16),
+            pltpu.VMEM((2, 32, HALF), BF16),
+            pltpu.VMEM((2, 4, 8, 2, 32, HALF), BF16),
             pltpu.VMEM((8, SHARE, HALF), BF16),
-            pltpu.VMEM((2, 4 * SHARE, HALF), F32),
+            pltpu.VMEM((2, 2 * SHARE, HALF), F32),
             pltpu.VMEM((2, 4, SHARE, HALF), BF16),
             pltpu.VMEM((8, SHARE, HALF), BF16),
             pltpu.VMEM((4, 8, SHARE), F32),
             pltpu.VMEM((8, 8, SHARE), F32),
             pltpu.VMEM((8, ROWS), F32),
             pltpu.VMEM((8, ROWS), F32),
-            pltpu.SemaphoreType.DMA((64,)),
-            pltpu.SemaphoreType.DMA((64,)),
+            pltpu.SemaphoreType.DMA((96,)),
+            pltpu.SemaphoreType.DMA((96,)),
             pltpu.SemaphoreType.DMA((40,)),
         ],
         compiler_params=pltpu.CompilerParams(
@@ -484,14 +514,27 @@
         ),
         name="step",
     )(
-        features,
-        labels.reshape(1, ROWS),
-        queries.reshape(2, SHARE, HALF),
-        bank,
-        old_conc.reshape(1, OWNED),
-        neg_index.reshape(64, 128),
-    )
-    new_bank, new_conc, loss, grad = outs
+        *(
+            pltpu.with_memory_space_constraint(a, pltpu.HBM)
+            for a in (
+                features,
+                labels.reshape(1, ROWS),
+                queries.reshape(2, SHARE, HALF),
+                bank,
+                old_conc.reshape(1, OWNED),
+                neg_index.reshape(64, 128),
+            )
+        )
+    )
+    new_bank, new_conc, loss, grad = pl.pallas_call(
+        hand_out,
+        out_shape=tuple(jax.ShapeDtypeStruct(o.shape, o.dtype) for o in outs),
+        in_specs=[vmem] * 4,
+        out_specs=(hbm,) * 4,
+        scratch_shapes=[pltpu.SemaphoreType.DMA((4,))],
+        compiler_params=pltpu.CompilerParams(vmem_limit_bytes=4 << 20),
+        name="hand_out",
+    )(*outs)
     return new_bank, new_conc.reshape(OWNED), loss.reshape(ROWS), grad
 
 

time: 99.9 us -> 86.8 us (0.87)
  local copies, waits for them, and re-layouts: 8.42 us -> 0 us
  Pallas kernels: 90.5 us -> 86.1 us
    unnamed x16 -> x0, local copies, waits for them, and re-layouts: 8.42 us -> none
    pallas_call x1, Pallas kernels: 90.5 us -> 84.8 us  [body(): pl.pallas_call(kernel, out_shape=(jax.ShapeDtypeStruct((OWNED, HALF), F32...]
    pallas_call x0 -> x1, Pallas kernels: none -> 1.31 us  [body(): pl.pallas_call(hand_out, out_shape=tuple((jax.ShapeDtypeStruct(o.shape, o...]
where the time goes in v3:
time: 86.8 us; the launch traced here: 86.7 us
  Pallas kernels  86.1 us (99%)
    pallas_call x1, Pallas kernels, body(): pl.pallas_call(kernel, out_shape=(jax.ShapeDtypeStruct((OWNED, HALF), F32...  84.8 us

profile of v3, /device:TPU:1, one launch (start us, length us, event | category | flops | bytes accessed | tf_op | source)
XLA Modules:
  0.0 86.7 jit_solution(1194498557895177306)
XLA Ops:
  0.6 84.8 %step.1 = (f32[1024,384]{1,0:T(8,128)S(1)}, f32[1,1024]{1,0:T(1,128)S(1)}, f32[1,256]{1,0:T(1,128)S(1)}, f32[256,384]{1,0:T(8,128)S(1)}) custom-call(bf16[256,384]{1,0:T(8,128)(2,1)} %feat_in.1, s32[1,256]{1,0:T(1,128)} %bitcast.9, bf16[2,128,384]{2,1,0:T(8,128)(2,1)} %bitcast.6, f32[1024,384]{1,0:T(8,128)} %bank_in.1, f32[1,1024]{1,0:T(1,128)} %bitcast.8, ...), custom_call_target="tpu_custom_call" | custom-call | tf_op jit(solution)/shard_map/step/pallas_call | solution.py:466
  85.4 1.3 %hand_out.1 = (f32[1024,384]{1,0:T(8,128)}, f32[1,1024]{1,0:T(1,128)}, f32[1,256]{1,0:T(1,128)}, f32[256,384]{1,0:T(8,128)}) custom-call(f32[1024,384]{1,0:T(8,128)S(1)} %get-tuple-element.12.refs_0_, f32[1,1024]{1,0:T(1,128)S(1)} %get-tuple-element.13.refs_1_, f32[1,256]{1,0:T(1,128)S(1)} %get-tuple-element.14.refs_2_, f32[256,384]{1,0:T(8,128)S(1)} %get-tuple-element.15.refs_3_), custom_call_target="tpu_custom_call" | custom-call | tf_op jit(solution)/shard_map/hand_out/pallas_call | solution.py:529

commit v4 on v3

--- a/solution.py
+++ b/solution.py
@@ -26,7 +26,7 @@
     return lax.rem(me + d, CHIPS)
 
 
-def blocks_start(src, dst, ssem, rsem, me):
+def blocks_start(src, dst, ssem, rsem, me, low=1, high=CHIPS):
     def go(d, _):
         o = peer(me, d)
         pltpu.make_async_remote_copy(
@@ -34,7 +34,7 @@
         ).start()
         return 0
 
-    lax.fori_loop(1, CHIPS, go, 0)
+    lax.fori_loop(low, high, go, 0)
 
 
 def wait_send(ref, ssem, rsem):
@@ -49,7 +49,7 @@
     ).wait_recv()
 
 
-def gather_rounds(mine, gathered, theirs, core, ssem, rsem, at_chip, pending):
+def gather_rounds(mine, gathered, theirs, core, ssem, rsem, at_chip, pending, handed):
     count = [0]
     lengths = {"y": LEN["y"], "z": LEN["z"]}
 
@@ -78,10 +78,9 @@
         ref = ref.at[off("y", y), off("z", z)]
         return ref if half is None else ref.at[half]
 
-    handed = []
-
     def hand_over(y, z):
-        handed.append((at(y, z, ref=theirs), send(at(y, z), at(y, z), mp=1 - core)))
+        i = send(at(y, z), at(y, z), mp=1 - core)
+        handed.append((y, lambda: arrived(at(y, z, ref=theirs), i)))
 
     flying = {}
 
@@ -129,16 +128,17 @@
     arrived(at(0, 4, 1), from_up)
     along_y(4)
     hand_over(0, 4)
+    yield
     for z in (-3, 3):
         on_y(z)
-    for z in (0, -1, 1):
+    end_y(0)
+    yield
+    on_y(4)
+    for z in (-1, 1):
         end_y(z)
-    on_y(4)
     yield
     for z in (-2, 2, -3, 3, 4):
         end_y(z)
-    for ref, i in handed:
-        arrived(ref, i)
 
 
 def as_column(row, n):
@@ -337,8 +337,9 @@
     swap.wait()
 
     pending = []
+    handed = []
     rounds = gather_rounds(
-        own, shards.at[core], shards.at[other], core, ag_send, ag_recv, at_chip, pending
+        own, shards.at[core], shards.at[other], core, ag_send, ag_recv, at_chip, pending, handed
     )
     next(rounds)
 
@@ -348,49 +349,56 @@
         hit = jnp.where(iota((TILE, OWNED), 1) == ids, 1.0, 0.0).astype(BF16)
         out = jnp.dot(hit, sv, preferred_element_type=F32).astype(BF16)
         back[k * 32 : (k + 1) * 32] = out.reshape(32, 8, HALF)
-    next(rounds)
-    blocks_start(
-        lambda o: back.at[o, six], lambda o: returned.at[o, six],
-        sem.at[4], sem.at[5], me,
-    )
     copy = pltpu.make_async_copy(back.at[me, six], returned.at[me, six], sem.at[18])
     copy.start()
     copy.wait()
-    for _ in rounds:
-        pass
-
-    seven = qf.at[pl.ds(0, 7)]
-    wait_recv(seven, sem.at[8], sem.at[9])
-    wait_send(seven, sem.at[8], sem.at[9])
+
+    def give_back(low, high):
+        blocks_start(
+            lambda o: back.at[o, six], lambda o: returned.at[o, six],
+            sem.at[4], sem.at[5], me, low, high,
+        )
+
     many = 2 * SHARE
     nt = (((1,), (1,)), ((), ()))
-    lane = iota((many, 128), 1)
-    for far in ((2, 1), (3, 0)):
-        chips = [lax.rem(x + d, 4) for d in far]
-        q0 = jnp.concatenate([qf[c] for c in chips], axis=0)
-        q1 = jnp.concatenate([qf[4 + c] for c in chips], axis=0)
-        top = jnp.full((many, 1), -3.0e38, F32)
-        sums = jnp.zeros((many, 1), F32)
-        for y in range(4):
-            k0 = shards[:, y, :, 0].reshape(2 * TILE, HALF)
-            k1 = shards[:, y, :, 1].reshape(2 * TILE, HALF)
+    parts = ((2, 1), (3, 0))
+    tops, totals = [None, None], [None, None]
+
+    def attend(y):
+        for plane, wait in handed:
+            if plane == y:
+                wait()
+        there = pl.ds(lax.rem(at_chip["y"] + y + 4, 4), 1)
+        k0 = shards[:, there, :, 0].reshape(2 * TILE, HALF)
+        k1 = shards[:, there, :, 1].reshape(2 * TILE, HALF)
+        for n, far in enumerate(parts):
+            chips = [lax.rem(x + d, 4) for d in far]
+            q0 = jnp.concatenate([qf[c] for c in chips], axis=0)
+            q1 = jnp.concatenate([qf[4 + c] for c in chips], axis=0)
             s = lax.dot_general(q0, k0, nt, preferred_element_type=F32)
             s = s + lax.dot_general(q1, k1, nt, preferred_element_type=F32)
-            higher = jnp.maximum(top, jnp.max(s, axis=1, keepdims=True))
-            shrink = jnp.exp(top - higher)
-            p = jnp.exp(s - higher)
-            sums = sums * shrink + jnp.sum(p, axis=1, keepdims=True)
+            high = jnp.max(s, axis=1, keepdims=True)
+            if tops[n] is not None:
+                high = jnp.maximum(tops[n], high)
+                shrink = jnp.exp(tops[n] - high)
+            p = jnp.exp(s - high)
+            total = jnp.sum(p, axis=1, keepdims=True)
             pb = p.astype(BF16)
             for h, kh in ((0, k0), (1, k1)):
                 more = jnp.dot(pb, kh, preferred_element_type=F32)
-                acc[h] = more if y == 0 else acc[h] * shrink + more
-            top = higher
-        both = jnp.transpose(jnp.where(lane == 0, top, sums))
-        for k, c in enumerate(chips):
+                acc[n, h] = more if tops[n] is None else acc[n, h] * shrink + more
+            totals[n] = total if tops[n] is None else totals[n] * shrink + total
+            tops[n] = high
+            if y == 2:
+                send_part(n, chips)
+
+    def send_part(n, chips):
+        both = jnp.transpose(jnp.where(iota((many, 128), 1) == 0, tops[n], totals[n]))
+        for k, (d, c) in enumerate(zip(parts[n], chips)):
             stats[c] = both[0:8, k * SHARE : (k + 1) * SHARE]
             for h in range(2):
-                acc16[h, c] = acc[h, k * SHARE : (k + 1) * SHARE].astype(BF16)
-        for d, c in zip(far, chips):
+                acc16[h, c] = acc[n, h, k * SHARE : (k + 1) * SHARE].astype(BF16)
+        for d, c in zip(parts[n], chips):
             if d == 0:
                 continue
             for h in range(2):
@@ -403,6 +411,23 @@
                     stats.at[c], stats_in.at[x * 2 + core], sem.at[27], sem.at[28],
                     device_id=to, device_id_type=MESH,
                 ).start()
+
+    for _ in range(4):
+        next(rounds)
+    give_back(1, 44)
+    next(rounds)
+    seven = qf.at[pl.ds(0, 7)]
+    wait_recv(seven, sem.at[8], sem.at[9])
+    wait_send(seven, sem.at[8], sem.at[9])
+    give_back(44, 86)
+    attend(0)
+    next(rounds)
+    give_back(86, CHIPS)
+    attend(-1)
+    attend(1)
+    for _ in rounds:
+        pass
+    attend(2)
     to_partner(stats.at[x], stats_in.at[x * 2 + core], 27).start()
     to_partner(acc16.at[other, x], acc_in.at[x * 2 + core], 25).start()
     keep = [
@@ -498,7 +523,7 @@
             pltpu.VMEM((2, 32, HALF), BF16),
             pltpu.VMEM((2, 4, 8, 2, 32, HALF), BF16),
             pltpu.VMEM((8, SHARE, HALF), BF16),
-            pltpu.VMEM((2, 2 * SHARE, HALF), F32),
+            pltpu.VMEM((2, 2, 2 * SHARE, HALF), F32),
             pltpu.VMEM((2, 4, SHARE, HALF), BF16),
             pltpu.VMEM((8, SHARE, HALF), BF16),
             pltpu.VMEM((4, 8, SHARE), F32),

time: 86.8 us -> 83.7 us (0.964)
  Pallas kernels: 86.1 us -> 82.9 us
    pallas_call x1, Pallas kernels: 84.8 us -> 81.6 us  [body(): pl.pallas_call(kernel, out_shape=(jax.ShapeDtypeStruct((OWNED, HALF), F32...]
where the time goes in v4:
time: 83.7 us; the launch traced here: 83.6 us
  Pallas kernels  82.9 us (99%)
    pallas_call x1, Pallas kernels, body(): pl.pallas_call(kernel, out_shape=(jax.ShapeDtypeStruct((OWNED, HALF), F32...  81.6 us

profile of v4, /device:TPU:1, one launch (start us, length us, event | category | flops | bytes accessed | tf_op | source)
XLA Modules:
  0.0 83.6 jit_solution(254599941762134506)
XLA Ops:
  0.6 81.6 %step.1 = (f32[1024,384]{1,0:T(8,128)S(1)}, f32[1,1024]{1,0:T(1,128)S(1)}, f32[1,256]{1,0:T(1,128)S(1)}, f32[256,384]{1,0:T(8,128)S(1)}) custom-call(bf16[256,384]{1,0:T(8,128)(2,1)} %feat_in.1, s32[1,256]{1,0:T(1,128)} %bitcast.9, bf16[2,128,384]{2,1,0:T(8,128)(2,1)} %bitcast.6, f32[1024,384]{1,0:T(8,128)} %bank_in.1, f32[1,1024]{1,0:T(1,128)} %bitcast.8, ...), custom_call_target="tpu_custom_call" | custom-call | tf_op jit(solution)/shard_map/step/pallas_call | solution.py:491
  82.3 1.3 %hand_out.1 = (f32[1024,384]{1,0:T(8,128)}, f32[1,1024]{1,0:T(1,128)}, f32[1,256]{1,0:T(1,128)}, f32[256,384]{1,0:T(8,128)}) custom-call(f32[1024,384]{1,0:T(8,128)S(1)} %get-tuple-element.12.refs_0_, f32[1,1024]{1,0:T(1,128)S(1)} %get-tuple-element.13.refs_1_, f32[1,256]{1,0:T(1,128)S(1)} %get-tuple-element.14.refs_2_, f32[256,384]{1,0:T(8,128)S(1)} %get-tuple-element.15.refs_3_), custom_call_target="tpu_custom_call" | custom-call | tf_op jit(solution)/shard_map/hand_out/pallas_call | solution.py:554

commit v5 on v4

--- a/solution.py
+++ b/solution.py
@@ -254,6 +254,24 @@
         lambda o: sent.at[o, six], lambda o: got.at[o, six, left],
         sem.at[2], sem.at[3], me,
     )
+    home = [
+        pltpu.make_async_copy(sent_ids.at[me, pl.ds(0, 1)], got_ids.at[me, pl.ds(0, 1)], sem.at[10]),
+        pltpu.make_async_copy(sent.at[me, six], got.at[me, six, left], sem.at[11]),
+    ]
+    for copy in home:
+        copy.start()
+    for copy in home:
+        copy.wait()
+    rest = pl.ds(0, CHIPS - 1)
+    wait_recv(got_ids.at[rest, pl.ds(0, 1)], sem.at[0], sem.at[1])
+
+    spread = jnp.broadcast_to(got_ids[:, 0:1, :], (CHIPS, 8, 128))
+    here = iota((CHIPS, 8, 128), 1) == iota((CHIPS, 8, 128), 2)
+    id_c = jnp.sum(jnp.where(here, spread, 0.0), axis=2, keepdims=True) - 1.0
+    wide[...] = jnp.broadcast_to(id_c, (CHIPS, 8, 128)).reshape(OWNED, 128)
+    id_row = jnp.transpose(wide[...])[0:1, :].astype(jnp.int32)
+    wait_recv(got.at[rest, six, left], sem.at[2], sem.at[3])
+
     x = at_chip["x"]
     for chip in beside:
         for c in range(2):
@@ -262,24 +280,8 @@
                 device_id={"dp": chip, "mp": c}, device_id_type=MESH,
             ).start()
     to_partner(q.at[other], qf.at[core * 4 + x], 8).start()
-    home = [
-        pltpu.make_async_copy(sent_ids.at[me, pl.ds(0, 1)], got_ids.at[me, pl.ds(0, 1)], sem.at[10]),
-        pltpu.make_async_copy(sent.at[me, six], got.at[me, six, left], sem.at[11]),
-        pltpu.make_async_copy(q.at[core], qf.at[core * 4 + x], sem.at[12]),
-    ]
-    for copy in home:
-        copy.start()
-    for copy in home:
-        copy.wait()
-    rest = pl.ds(0, CHIPS - 1)
-    wait_recv(got_ids.at[rest, pl.ds(0, 1)], sem.at[0], sem.at[1])
-
-    spread = jnp.broadcast_to(got_ids[:, 0:1, :], (CHIPS, 8, 128))
-    here = iota((CHIPS, 8, 128), 1) == iota((CHIPS, 8, 128), 2)
-    id_c = jnp.sum(jnp.where(here, spread, 0.0), axis=2, keepdims=True) - 1.0
-    wide[...] = jnp.broadcast_to(id_c, (CHIPS, 8, 128)).reshape(OWNED, 128)
-    id_row = jnp.transpose(wide[...])[0:1, :].astype(jnp.int32)
-    wait_recv(got.at[rest, six, left], sem.at[2], sem.at[3])
+    stay = pltpu.make_async_copy(q.at[core], qf.at[core * 4 + x], sem.at[12])
+    stay.start()
 
     for copy in reads[3:]:
         copy.wait()
@@ -412,17 +414,20 @@
                     device_id=to, device_id_type=MESH,
                 ).start()
 
-    for _ in range(4):
+    for low in (1, 15, 29):
         next(rounds)
-    give_back(1, 44)
+        give_back(low, low + 14)
+    next(rounds)
+    give_back(43, 71)
     next(rounds)
     seven = qf.at[pl.ds(0, 7)]
     wait_recv(seven, sem.at[8], sem.at[9])
     wait_send(seven, sem.at[8], sem.at[9])
-    give_back(44, 86)
+    stay.wait()
+    give_back(71, 99)
     attend(0)
     next(rounds)
-    give_back(86, CHIPS)
+    give_back(99, CHIPS)
     attend(-1)
     attend(1)
     for _ in rounds:

time: 83.7 us -> 84.2 us (level)
  no operation moved by 1% of the time
where the time goes in v5:
time: 84.2 us; the launch traced here: 84.1 us
  Pallas kernels  83.5 us (99%)
    pallas_call x1, Pallas kernels, body(): pl.pallas_call(kernel, out_shape=(jax.ShapeDtypeStruct((OWNED, HALF), F32...  82.2 us

profile of v5, /device:TPU:1, one launch (start us, length us, event | category | flops | bytes accessed | tf_op | source)
XLA Modules:
  0.0 84.1 jit_solution(3277243645308130465)
XLA Ops:
  0.6 82.2 %step.1 = (f32[1024,384]{1,0:T(8,128)S(1)}, f32[1,1024]{1,0:T(1,128)S(1)}, f32[1,256]{1,0:T(1,128)S(1)}, f32[256,384]{1,0:T(8,128)S(1)}) custom-call(bf16[256,384]{1,0:T(8,128)(2,1)} %feat_in.1, s32[1,256]{1,0:T(1,128)} %bitcast.9, bf16[2,128,384]{2,1,0:T(8,128)(2,1)} %bitcast.6, f32[1024,384]{1,0:T(8,128)} %bank_in.1, f32[1,1024]{1,0:T(1,128)} %bitcast.8, ...), custom_call_target="tpu_custom_call" | custom-call | tf_op jit(solution)/shard_map/step/pallas_call | solution.py:496
  82.8 1.3 %hand_out.1 = (f32[1024,384]{1,0:T(8,128)}, f32[1,1024]{1,0:T(1,128)}, f32[1,256]{1,0:T(1,128)}, f32[256,384]{1,0:T(8,128)}) custom-call(f32[1024,384]{1,0:T(8,128)S(1)} %get-tuple-element.12.refs_0_, f32[1,1024]{1,0:T(1,128)S(1)} %get-tuple-element.13.refs_1_, f32[1,256]{1,0:T(1,128)S(1)} %get-tuple-element.14.refs_2_, f32[256,384]{1,0:T(8,128)S(1)} %get-tuple-element.15.refs_3_), custom_call_target="tpu_custom_call" | custom-call | tf_op jit(solution)/shard_map/hand_out/pallas_call | solution.py:559

commit v6 on v5

--- a/solution.py
+++ b/solution.py
@@ -78,9 +78,10 @@
         ref = ref.at[off("y", y), off("z", z)]
         return ref if half is None else ref.at[half]
 
-    def hand_over(y, z):
-        i = send(at(y, z), at(y, z), mp=1 - core)
-        handed.append((y, lambda: arrived(at(y, z, ref=theirs), i)))
+    def hand_over(y, z=None):
+        mine, its = (r.at[off("y", y)] if z is None else at(y, z, ref=r) for r in (gathered, theirs))
+        i = send(mine, mine, mp=1 - core)
+        handed.append((y, lambda: arrived(its, i)))
 
     flying = {}
 
@@ -93,8 +94,6 @@
         right = send(at(-1, z, 0), at(-1, z, 0), dp=chip("y", 1))
         arrived(at(1, z), flying[z][1])
         flying[z] = (right, send(at(1, z, 1), at(1, z, 1), dp=chip("y", -1)))
-        hand_over(-1, z)
-        hand_over(1, z)
 
     def end_y(z):
         arrived(at(2, z, 0), flying[z][0])
@@ -109,7 +108,6 @@
     local = pltpu.make_async_copy(mine, at(0, 0), ssem.at[i])
     local.start()
     local.wait()
-    hand_over(0, 0)
     yield
     for s in (1, 2, 3):
         part = (0, 1) if s == 3 else (None, None)
@@ -119,21 +117,21 @@
         from_up = send(at(0, s, part[1]), at(0, s, part[1]), dp=down)
         along_y(-s)
         along_y(s)
-        hand_over(0, -s)
-        hand_over(0, s)
         for z in ((0,), (-1, 1), (-2, 2))[s - 1]:
             on_y(z)
         yield
     arrived(at(0, 4, 0), from_down)
     arrived(at(0, 4, 1), from_up)
     along_y(4)
-    hand_over(0, 4)
+    hand_over(0)
     yield
     for z in (-3, 3):
         on_y(z)
     end_y(0)
     yield
     on_y(4)
+    hand_over(-1)
+    hand_over(1)
     for z in (-1, 1):
         end_y(z)
     yield
@@ -151,7 +149,7 @@
     new_bank, new_conc, loss, grad,
     feat, labels, q, bank, old_conc, negs,
     sent, sent_ids, got, got_ids, back, returned, route, wide,
-    d2_mine, d2_theirs, nb16, scaled, count_of, conc_of, mine, own,
+    d2_mine, d2_theirs, nb16, scaled, count_of, conc_of, mine,
     shards, qf, acc, acc16, acc_in, stats, stats_in, pos_mine, pos_theirs,
     ag_send, ag_recv, sem,
 ):
@@ -328,22 +326,15 @@
 
     sv = scaled[...]
     hit = jnp.where(iota((128, OWNED), 1) == want, 1.0, 0.0).astype(BF16)
-    mine[...] = jnp.dot(hit, sv, preferred_element_type=F32).astype(BF16).reshape(4, 32, HALF)
-    base = lax.rem(me, 2) * 2
-    swap = to_partner(mine.at[base + other], own.at[core], 21)
-    swap.start()
-    keep = pltpu.make_async_copy(mine.at[base + core], own.at[core], sem.at[15])
-    keep.start()
-    keep.wait()
-    new_conc[...] = jnp.transpose(conc_of[...])[0:1, :]
-    swap.wait()
-
+    mine[...] = jnp.dot(hit, sv, preferred_element_type=F32).astype(BF16).reshape(2, 2, 32, HALF)
     pending = []
     handed = []
     rounds = gather_rounds(
-        own, shards.at[core], shards.at[other], core, ag_send, ag_recv, at_chip, pending, handed
+        mine.at[lax.rem(me, 2)], shards.at[core], shards.at[other], core,
+        ag_send, ag_recv, at_chip, pending, handed,
     )
     next(rounds)
+    new_conc[...] = jnp.transpose(conc_of[...])[0:1, :]
 
     for k in range(OWNED // TILE):
         rows = pl.ds(k * TILE, TILE)
@@ -371,8 +362,8 @@
             if plane == y:
                 wait()
         there = pl.ds(lax.rem(at_chip["y"] + y + 4, 4), 1)
-        k0 = shards[:, there, :, 0].reshape(2 * TILE, HALF)
-        k1 = shards[:, there, :, 1].reshape(2 * TILE, HALF)
+        k0 = shards[0, there].reshape(2 * TILE, HALF)
+        k1 = shards[1, there].reshape(2 * TILE, HALF)
         for n, far in enumerate(parts):
             chips = [lax.rem(x + d, 4) for d in far]
             q0 = jnp.concatenate([qf[c] for c in chips], axis=0)
@@ -414,20 +405,18 @@
                     device_id=to, device_id_type=MESH,
                 ).start()
 
-    for low in (1, 15, 29):
+    for _ in range(4):
         next(rounds)
-        give_back(low, low + 14)
-    next(rounds)
-    give_back(43, 71)
+    give_back(1, 44)
     next(rounds)
     seven = qf.at[pl.ds(0, 7)]
     wait_recv(seven, sem.at[8], sem.at[9])
     wait_send(seven, sem.at[8], sem.at[9])
     stay.wait()
-    give_back(71, 99)
+    give_back(44, 86)
     attend(0)
     next(rounds)
-    give_back(99, CHIPS)
+    give_back(86, CHIPS)
     attend(-1)
     attend(1)
     for _ in rounds:
@@ -524,8 +513,7 @@
             pltpu.VMEM((OWNED, HALF), BF16),
             pltpu.VMEM((OWNED, 128), F32),
             pltpu.VMEM((OWNED, 128), F32),
-            pltpu.VMEM((4, 32, HALF), BF16),
-            pltpu.VMEM((2, 32, HALF), BF16),
+            pltpu.VMEM((2, 2, 32, HALF), BF16),
             pltpu.VMEM((2, 4, 8, 2, 32, HALF), BF16),
             pltpu.VMEM((8, SHARE, HALF), BF16),
             pltpu.VMEM((2, 2, 2 * SHARE, HALF), F32),

time: 84.2 us -> 83 us (0.986)
  Pallas kernels: 83.5 us -> 82.3 us
    pallas_call x1, Pallas kernels: 82.2 us -> 80.9 us  [body(): pl.pallas_call(kernel, out_shape=(jax.ShapeDtypeStruct((OWNED, HALF), F32...]
where the time goes in v6:
time: 83 us; the launch traced here: 82.9 us
  Pallas kernels  82.3 us (99%)
    pallas_call x1, Pallas kernels, body(): pl.pallas_call(kernel, out_shape=(jax.ShapeDtypeStruct((OWNED, HALF), F32...  80.9 us

profile of v6, /device:TPU:1, one launch (start us, length us, event | category | flops | bytes accessed | tf_op | source)
XLA Modules:
  0.0 82.9 jit_solution(3504894900450637527)
XLA Ops:
  0.6 80.9 %step.1 = (f32[1024,384]{1,0:T(8,128)S(1)}, f32[1,1024]{1,0:T(1,128)S(1)}, f32[1,256]{1,0:T(1,128)S(1)}, f32[256,384]{1,0:T(8,128)S(1)}) custom-call(bf16[256,384]{1,0:T(8,128)(2,1)} %feat_in.1, s32[1,256]{1,0:T(1,128)} %bitcast.9, bf16[2,128,384]{2,1,0:T(8,128)(2,1)} %bitcast.6, f32[1024,384]{1,0:T(8,128)} %bank_in.1, f32[1,1024]{1,0:T(1,128)} %bitcast.8, ...), custom_call_target="tpu_custom_call" | custom-call | tf_op jit(solution)/shard_map/step/pallas_call | solution.py:485
  81.6 1.3 %hand_out.1 = (f32[1024,384]{1,0:T(8,128)}, f32[1,1024]{1,0:T(1,128)}, f32[1,256]{1,0:T(1,128)}, f32[256,384]{1,0:T(8,128)}) custom-call(f32[1024,384]{1,0:T(8,128)S(1)} %get-tuple-element.12.refs_0_, f32[1,1024]{1,0:T(1,128)S(1)} %get-tuple-element.13.refs_1_, f32[1,256]{1,0:T(1,128)S(1)} %get-tuple-element.14.refs_2_, f32[256,384]{1,0:T(8,128)S(1)} %get-tuple-element.15.refs_3_), custom_call_target="tpu_custom_call" | custom-call | tf_op jit(solution)/shard_map/hand_out/pallas_call | solution.py:547
